TPU v7x, 256 devices: a whole 4x4x8 slice. The times are simulated.
256 devices in a mesh: seq: 128 (over x_lo, y, z, core), head: 2 (over x_hi).
Axes of the slice: x: 4 (x_hi: 2, x_lo: 2; x = x_hi * 2 + x_lo), y: 4, z: 8, core: 2. Of those that a mesh axis runs over, the one named last changes fastest.
Arguments:
- queries: bfloat16 [16384, 3072], P('seq', 'head'), may hold values from -6 to 6
- keys: bfloat16 [16384, 3072], P('seq', 'head'), may hold values from -6 to 6
- values: bfloat16 [16384, 3072], P('seq', 'head'), may hold values from -6 to 6
- cache_k: bfloat16 [2048, 3072], P('seq', 'head'), may hold values from -6 to 6
- cache_v: bfloat16 [2048, 3072], P('seq', 'head'), may hold values from -6 to 6
- sink_k: bfloat16 [8, 3072], P(None, 'head'), may hold values from -6 to 6
- sink_v: bfloat16 [8, 3072], P(None, 'head'), may hold values from -6 to 6
- suffix_lengths: int32 [32], replicated, may hold values from 1 to 1024, 16384 in all
- request_group: int32 [32], replicated, may hold values from 0 to 1
- w_out: bfloat16 [3072, 3072], P('head'), may hold values from -0.109375 to 0.109375
Outputs:
- projected: bfloat16 [3072, 16384], P('head', 'seq')
All inputs are finite; a program needn't handle non-finite values.
Results may differ from a plain program's by a relative error of at most 0.011.
Values may be sent and summed in bfloat16 or wider, within the bound.
No kernel may reach another device: no remote copies, remote signals or barrier semaphores. Data moves between devices by JAX's collectives and lax.ppermute only.
A program may use at most 128 MiB of HBM per device.

v0:
```python
import functools
import math

import jax
import jax.numpy as jnp
from jax import lax
from jax.experimental import pallas as pl
from jax.experimental.pallas import tpu as pltpu
from jax.sharding import PartitionSpec as P

HD = 96
W = 1024
SINKS = 4
G = 2
RING = 16
BLK = 128
QB = 256
CH = 256
LANES = 128
FAR = 1 << 28
LOW = -1e30
VMEM_LIMIT = 24 << 20
PIECE = 256


def pack_kernel(k_ref, v_ref, ck_ref, cv_ref, out_ref):
    heads = k_ref.shape[1] // HD
    for which, ref in enumerate((k_ref, v_ref)):
        turned = ref[...].T
        for p in range(heads):
            out_ref[p, which * HD : (which + 1) * HD, :] = turned[p * HD : (p + 1) * HD, :]
    rows = ck_ref.shape[0]
    fill = jnp.zeros((rows, LANES - HD), ck_ref.dtype)
    for which, ref in enumerate((ck_ref, cv_ref)):
        for p in range(heads):
            piece = jnp.concatenate([ref[:, p * HD : (p + 1) * HD], fill], axis=1)
            base = 2 * HD + which * rows
            out_ref[p, base : base + rows, :] = piece


def gather_facts(place, lengths, groups, need, blocks):
    base = place[0] * RING * BLK
    own = RING * BLK
    for b in range((1 + G) * blocks):
        need[b] = FAR
    need[(1 + G) * blocks] = place[0]

    def one_request(r, carry):
        start, start_col, group_col = carry
        length = lengths[r]
        group = groups[r]
        first = jnp.where(start < base, 0, (start - base) // QB)
        last = jnp.minimum((start + length - 1 - base) // QB, blocks - 1)

        def mark(b, _):
            need[b] = jnp.minimum(need[b], start)
            offset = jnp.maximum(base + b * QB - start, 0)
            at = (1 + group) * blocks + b
            need[at] = jnp.minimum(need[at], offset)
            return 0

        @pl.when((start < base + own) & (start + length > base))
        def _():
            lax.fori_loop(first, last + 1, mark, 0)

        row = lax.broadcasted_iota(jnp.int32, start_col.shape, 0)
        start_col = jnp.where(row == r, start, start_col)
        group_col = jnp.where(row == r, group, group_col)
        return (start + length, start_col, group_col)

    reqs = lengths.shape[0]
    column = jnp.zeros((reqs, QB), jnp.int32)
    _, start_col, group_col = lax.fori_loop(0, reqs, one_request, (jnp.int32(0), column, column))
    return base, start_col, group_col


def query_facts(index, start_col, group_col):
    begun = start_col <= index
    start_q = jnp.max(jnp.where(begun, start_col, 0), axis=0, keepdims=True)
    here = begun & (start_col == start_q)
    group_q = jnp.max(jnp.where(here, group_col, 0), axis=0, keepdims=True)
    return jnp.maximum(start_q, index - (W - 1)), index - start_q, group_q


def turn(piece):
    pad = jnp.zeros((LANES - HD, BLK), jnp.bfloat16)
    return jnp.concatenate([piece, pad], axis=0).T


def query_block(query_ref, b):
    q_t = jnp.concatenate([query_ref[2 * b], query_ref[2 * b + 1]], axis=1)
    return jnp.concatenate([q_t, jnp.zeros((LANES - HD, QB), jnp.bfloat16)], axis=0)


def values(val_ref, at):
    slot = at // BLK
    return jnp.concatenate([val_ref[slot], val_ref[slot + 1]], axis=1)


def dot(a, b):
    return jnp.dot(a, b, preferred_element_type=jnp.float32)


FACTOR = (1.0 / math.sqrt(HD)) * math.log2(math.e)


def prep_kernel(own_ref, key_ref, last_ref):
    for j in range(RING // 2):
        last_ref[j] = own_ref[RING // 2 + j, 0 : 2 * HD, :]
    for j in range(RING):
        key_ref[j * BLK : (j + 1) * BLK, :] = turn(own_ref[j, 0:HD, :])


def pack_query_kernel(
    place, lengths, groups, q_ref, sk_ref, sv_ref, query_ref, sink_ref, low_ref, need
):
    turned = q_ref[...].T
    for p in range(q_ref.shape[1] // HD):
        query_ref[p] = turned[p * HD : (p + 1) * HD, :]
    width = sk_ref.shape[1]
    column = lax.broadcasted_iota(jnp.int32, (width, LANES), 0)
    lane = lax.broadcasted_iota(jnp.int32, (width, LANES), 1)
    pick = ((column == place[1] * HD + lane) & (lane < HD)).astype(jnp.float32).astype(jnp.bfloat16)
    for which, ref in enumerate((sk_ref, sv_ref)):
        piece = jnp.dot(ref[...], pick, preferred_element_type=jnp.float32)
        piece = jnp.concatenate([piece, jnp.zeros_like(piece)], axis=0)
        sink_ref[which * 16 : (which + 1) * 16, :] = piece.astype(jnp.bfloat16)
    own = RING * BLK
    blocks = own // QB
    cache_at = own
    base, start_col, group_col = gather_facts(place, lengths, groups, need, blocks)
    lane = lax.broadcasted_iota(jnp.int32, (1, QB), 1)
    for b in range(blocks):
        index = base + b * QB + lane
        low_q, offset, group_q = query_facts(index, start_col, group_col)
        low_ref[b, 0:1, :] = low_q - base
        for g in range(G):
            low_ref[b, 1 + g : 2 + g, :] = jnp.where(
                group_q == g, cache_at + g * W + offset + 1, FAR
            )
        low_ref[b, 1 + G : 2 + G, :] = jnp.full((1, QB), FAR, jnp.int32)
        low_ref[b, 2 + G : 3 + G, :] = group_q


def fold(rows, how):
    return how(rows.reshape(rows.shape[0] // 8, 8, QB), axis=0)


def visit(total, where_is, key_ref, val_ref, low_of, q_t, state, buffers):
    s_even, s_odd, p_even, p_odd = buffers
    row_iota = lax.broadcasted_iota(jnp.int32, (PIECE, QB), 0)
    pieces = [slice(n * PIECE, (n + 1) * PIECE) for n in range(CH // PIECE)]

    def scores(j, ref):
        at, kind = where_is(j)
        low = low_of(kind) - at
        peak = None
        for n, rows in enumerate(pieces):
            s = dot(key_ref[pl.ds(at + n * PIECE, PIECE), :], q_t)
            s = jnp.where(row_iota >= low - n * PIECE, s, LOW)
            ref[rows, :] = s
            high = fold(s, jnp.max)
            peak = high if peak is None else jnp.maximum(peak, high)
        return peak, at

    def weigh(s_ref, p_ref, peak, top, den):
        new = jnp.maximum(top, jnp.max(peak, axis=0, keepdims=True))
        fade = jnp.exp2((top - new) * FACTOR)
        den = den * fade
        for rows in pieces:
            p = jnp.exp2((s_ref[rows, :] - new) * FACTOR)
            den = den + fold(p, jnp.sum)
            p_ref[rows, :] = p.astype(jnp.bfloat16)
        return new, fade, den

    top, den, acc, before = state
    peak, at = scores(0, s_even)

    def step(j, state):
        top, den, acc, before, peak, at = state
        next_peak, next_at = scores(2 * j + 1, s_odd)
        acc = acc + dot(values(val_ref, before), p_odd[...])
        top, fade, den = weigh(s_even, p_even, peak, top, den)
        acc = acc * fade + dot(values(val_ref, at), p_even[...])
        peak, last_at = scores(2 * j + 2, s_even)
        top, fade, den = weigh(s_odd, p_odd, next_peak, top, den)
        acc = acc * fade
        return (top, den, acc, next_at, peak, last_at)

    top, den, acc, before, _, _ = lax.fori_loop(
        0, (total + 1) // 2, step, (top, den, acc, before, peak, at)
    )
    return top, den, acc + dot(values(val_ref, before), p_odd[...])


def attend_kernel(
    need, low_ref, sink_ref, query_ref, own_ref, turned_ref, *rest, rings
):
    caches = rest[:rings]
    upper_ref, stat_ref, acc_ref, key_ref, val_ref = rest[rings : rings + 5]
    buffers = rest[rings + 5 :]
    own = RING * BLK
    blocks = own // QB
    ring = need[(1 + G) * blocks]
    base = ring * own
    key_ref[0:own, :] = turned_ref[...]
    for j in range(RING):
        val_ref[j] = own_ref[j, HD : 2 * HD, :]
    rows = RING * 16
    for k in range(rings):
        source = lax.rem(lax.rem(ring, 4) + k % 4, 4) + 4 * lax.rem(ring // 4 + k // 4, 2)
        piece = caches[k][...]
        at = pl.multiple_of(own + source * rows, rows)
        key_ref[pl.ds(at, rows), :] = piece[:, 0:16, :].reshape(rows, LANES)
        turned = piece[:, 16:32, :].reshape(rows, LANES).T
        for half in range(rows // BLK):
            val_ref[at // BLK + half] = turned[0:HD, half * BLK : (half + 1) * BLK]
    lane = lax.broadcasted_iota(jnp.int32, (1, QB), 1)
    row_iota = lax.broadcasted_iota(jnp.int32, (CH, QB), 0)
    sink_row = lax.broadcasted_iota(jnp.int32, (16, QB), 0)
    sink_v = sink_ref[16:32, :].T[0:HD, :]

    def one_block(b, _):
        low_suffix = low_ref[b, 0:1, :]
        group_q = low_ref[b, 2 + G : 3 + G, :]
        q_t = query_block(query_ref, b)
        at0 = pl.multiple_of(b * QB, CH)
        s_d = dot(key_ref[pl.ds(at0, CH), :], q_t)
        s_d = jnp.where((row_iota >= low_suffix - at0) & (row_iota <= lane), s_d, LOW)
        s_s = dot(sink_ref[0:16, :], q_t)
        s_s = jnp.where((sink_row // SINKS == group_q) & (sink_row < G * SINKS), s_s, LOW)
        top = jnp.maximum(jnp.max(s_d, axis=0, keepdims=True), jnp.max(s_s, axis=0, keepdims=True))
        p_d = jnp.exp2((s_d - top) * FACTOR)
        p_s = jnp.exp2((s_s - top) * FACTOR)
        den = fold(p_d, jnp.sum) + fold(p_s, jnp.sum)
        buffers[3][...] = p_d.astype(jnp.bfloat16)
        acc = dot(sink_v, p_s.astype(jnp.bfloat16))

        first = jnp.maximum(jnp.maximum(need[b] - base, b * QB - (W - 1)), 0) // CH
        n_suffix = b - first
        c0 = [jnp.minimum((need[(1 + g) * blocks + b] + 1) // CH, W // CH) for g in range(G)]
        n0, n1 = [W // CH - c for c in c0]
        total = n_suffix + n0 + n1

        def where_is(j):
            in0 = j - n_suffix
            in1 = in0 - n0
            at = jnp.where(
                in0 < 0,
                (first + j) * CH,
                jnp.where(
                    in1 < 0,
                    own + (c0[0] + in0) * CH,
                    jnp.where(j < total, own + W + (c0[1] + in1) * CH, 0),
                ),
            )
            kind = jnp.where(in0 < 0, 0, jnp.where(in1 < 0, 1, jnp.where(j < total, 2, 3)))
            return pl.multiple_of(at, CH), kind

        def low_of(kind):
            return low_ref[b, pl.ds(kind, 1), :]

        state = (top, den, acc, at0)
        top, den, acc = visit(total, where_is, key_ref, val_ref, low_of, q_t, state, buffers)

        @pl.when(b < blocks // 2)
        def _():
            stat_ref[b, 0:8, :] = jnp.broadcast_to(top, (8, QB))
            stat_ref[b, 8:16, :] = den
            acc_ref[b] = acc

        @pl.when(b >= blocks // 2)
        def _():
            done = (acc / jnp.sum(den, axis=0, keepdims=True)).astype(jnp.bfloat16)
            upper_ref[2 * b - RING // 2] = done[:, 0:BLK]
            upper_ref[2 * b + 1 - RING // 2] = done[:, BLK:QB]

        return 0

    lax.fori_loop(0, blocks, one_block, 0)


def window_kernel(
    need, low_ref, query_ref, win_ref, upper_ref, stat_ref, acc_ref, out_ref,
    key_ref, val_ref, *buffers,
):
    blocks = RING * BLK // QB
    base = need[(1 + G) * blocks] * RING * BLK
    for j in range(RING // 2):
        key_ref[j * BLK : (j + 1) * BLK, :] = turn(win_ref[j, 0:HD, :])
        val_ref[j] = win_ref[j, HD : 2 * HD, :]
        out_ref[RING // 2 + j] = upper_ref[j]

    def one_block(b, _):
        q_t = query_block(query_ref, b)
        first = jnp.maximum(need[b] - base, b * QB - (W - 1)) + W
        first = jnp.minimum(first // CH, W // CH)
        total = W // CH - first

        def where_is(j):
            at = jnp.where(j < total, (first + j) * CH, 0)
            return pl.multiple_of(at, CH), jnp.where(j < total, 0, 1 + G)

        def low_of(kind):
            return low_ref[b, pl.ds(kind, 1), :] + jnp.where(kind == 0, W, 0)

        buffers[3][...] = jnp.zeros((CH, QB), jnp.bfloat16)
        state = (stat_ref[b, 0:1, :], stat_ref[b, 8:16, :], acc_ref[b], jnp.int32(0))
        _, den, acc = visit(total, where_is, key_ref, val_ref, low_of, q_t, state, buffers)
        done = (acc / jnp.sum(den, axis=0, keepdims=True)).astype(jnp.bfloat16)
        out_ref[2 * b] = done[:, 0:BLK]
        out_ref[2 * b + 1] = done[:, BLK:QB]
        return 0

    lax.fori_loop(0, blocks // 2, one_block, 0)


def project_kernel(side, attn_ref, w_ref, out_ref, half_ref, sum_ref, arrived):
    features = half_ref.shape[1]
    columns = pl.ds(pl.multiple_of(side[0] * features, features), features)
    parts = arrived.shape[0]
    tall = half_ref.shape[0] // parts
    loads = []
    for n in range(parts):
        rows = pl.ds(n * tall, tall)
        loads.append(
            pltpu.make_async_copy(w_ref.at[rows, columns], half_ref.at[rows, :], arrived.at[n])
        )
    for load in loads:
        load.start()
    turned = attn_ref[...].T
    for n in range(parts):
        loads[n].wait()
        at = slice(n * tall, (n + 1) * tall)
        part = dot(turned[:, at], half_ref[at, :])
        if n == 0:
            sum_ref[...] = part
        elif n < parts - 1:
            sum_ref[...] += part
        else:
            out_ref[...] = (sum_ref[...] + part).T.astype(out_ref.dtype)


def project(side, attn_t, w_out, dtype):
    width, rows = attn_t.shape
    features = w_out.shape[1] // 2
    return pl.pallas_call(
        project_kernel,
        out_shape=jax.ShapeDtypeStruct((features, rows), dtype),
        in_specs=[smem(), vmem(), pl.BlockSpec(memory_space=pltpu.HBM)],
        out_specs=vmem(),
        scratch_shapes=[
            pltpu.VMEM((width, features), jnp.bfloat16),
            pltpu.VMEM((rows, features), jnp.float32),
            pltpu.SemaphoreType.DMA((6,)),
        ],
        cost_estimate=pl.CostEstimate(
            flops=2 * width * features * rows,
            bytes_accessed=2 * width * features,
            transcendentals=0,
        ),
        compiler_params=pltpu.CompilerParams(vmem_limit_bytes=50 << 20),
        name="project",
    )(side.reshape(1), attn_t, w_out)


def vmem():
    return pl.BlockSpec(memory_space=pltpu.VMEM)


def smem():
    return pl.BlockSpec(memory_space=pltpu.SMEM)


def shards(
    queries, keys, values, cache_k, cache_v, sink_k, sink_v, suffix_lengths, request_group, w_out
):
    rows, width = queries.shape
    heads = width // HD
    seq = lax.axis_size("seq")
    rings = seq // RING
    device = lax.axis_index("seq")
    half = lax.axis_index("head")
    packed = pl.pallas_call(
        pack_kernel,
        out_shape=jax.ShapeDtypeStruct((heads, 2 * HD + 32, LANES), jnp.bfloat16),
        in_specs=[vmem()] * 4,
        out_specs=vmem(),
        name="pack",
    )(keys, values, cache_k, cache_v)
    own = RING * BLK
    blocks = own // QB
    place = jnp.stack([device // RING, device % RING]).astype(jnp.int32)
    packed_q, sinks, lows, need = pl.pallas_call(
        pack_query_kernel,
        out_shape=(
            jax.ShapeDtypeStruct((heads, HD, LANES), jnp.bfloat16),
            jax.ShapeDtypeStruct((32, LANES), jnp.bfloat16),
            jax.ShapeDtypeStruct((blocks, 8, QB), jnp.int32),
            jax.ShapeDtypeStruct(((1 + G) * blocks + 1,), jnp.int32),
        ),
        in_specs=[smem()] * 3 + [vmem()] * 3,
        out_specs=(vmem(), vmem(), vmem(), smem()),
        cost_estimate=pl.CostEstimate(flops=1 << 20, bytes_accessed=1 << 21, transcendentals=0),
        compiler_params=pltpu.CompilerParams(vmem_limit_bytes=VMEM_LIMIT),
        name="pack_query",
    )(place, suffix_lengths, request_group, queries, sink_k, sink_v)
    members = [[r * RING + i for i in range(RING)] for r in range(rings)]

    def trade(array, groups):
        return lax.all_to_all(array, "seq", 0, 0, axis_index_groups=groups, tiled=True)

    mine = trade(packed, members)
    mine_q = trade(packed_q, members)
    cache = mine[:, 2 * HD :, :]

    def send(array, dx, dy):
        pairs = []
        for r in range(rings):
            to = (r % 4 + dy) % 4 + 4 * ((r // 4 + dx) % 2)
            pairs += [(r * RING + i, to * RING + i) for i in range(RING)]
        return lax.ppermute(array, "seq", pairs)

    near_y = send(cache, 0, 3)
    near_x = send(cache, 1, 0)
    back_y = send(cache, 0, 1)
    far_y = send(cache, 0, 2)
    near_xy = send(near_x, 0, 3)
    back_xy = send(back_y, 1, 0)
    far_xy = send(far_y, 1, 0)
    caches = [cache, near_y, far_y, back_y, near_x, near_xy, far_xy, back_xy]
    turned, last = pl.pallas_call(
        prep_kernel,
        out_shape=(
            jax.ShapeDtypeStruct((own, LANES), jnp.bfloat16),
            jax.ShapeDtypeStruct((RING // 2, 2 * HD, LANES), jnp.bfloat16),
        ),
        in_specs=[vmem()],
        out_specs=(vmem(), vmem()),
        cost_estimate=pl.CostEstimate(
            flops=1 << 20, bytes_accessed=1 << 22, transcendentals=0
        ),
        compiler_params=pltpu.CompilerParams(vmem_limit_bytes=VMEM_LIMIT),
        name="prep",
    )(mine)
    window = lax.ppermute(last, "seq", [(s, s + RING) for s in range(seq - RING)])
    buffers = [pltpu.VMEM((CH, QB), jnp.float32)] * 2 + [pltpu.VMEM((CH, QB), jnp.bfloat16)] * 2
    upper, stats, sums = pl.pallas_call(
        functools.partial(attend_kernel, rings=rings),
        out_shape=(
            jax.ShapeDtypeStruct((RING // 2, HD, BLK), jnp.bfloat16),
            jax.ShapeDtypeStruct((blocks // 2, 16, QB), jnp.float32),
            jax.ShapeDtypeStruct((blocks // 2, HD, QB), jnp.float32),
        ),
        in_specs=[smem()] + [vmem()] * (5 + rings),
        out_specs=(vmem(), vmem(), vmem()),
        scratch_shapes=[
            pltpu.VMEM((own + G * W, LANES), jnp.bfloat16),
            pltpu.VMEM(((own + G * W) // BLK, HD, BLK), jnp.bfloat16),
            *buffers,
        ],
        cost_estimate=pl.CostEstimate(
            flops=own * 2 * W * HD * 4, bytes_accessed=1 << 22, transcendentals=own * 2 * W
        ),
        compiler_params=pltpu.CompilerParams(vmem_limit_bytes=VMEM_LIMIT),
        name="attend",
    )(need, lows, sinks, mine_q, mine, turned, *caches)
    attn = pl.pallas_call(
        window_kernel,
        out_shape=jax.ShapeDtypeStruct((RING, HD, BLK), jnp.bfloat16),
        in_specs=[smem()] + [vmem()] * 6,
        out_specs=vmem(),
        scratch_shapes=[
            pltpu.VMEM((W, LANES), jnp.bfloat16),
            pltpu.VMEM((W // BLK, HD, BLK), jnp.bfloat16),
            *buffers,
        ],
        compiler_params=pltpu.CompilerParams(vmem_limit_bytes=VMEM_LIMIT),
        name="window",
    )(need, lows, mine_q, window, upper, stats, sums)
    attn_t = trade(attn, members).reshape(width, rows)
    give = project(1 - half, attn_t, w_out, jnp.bfloat16)
    got = lax.ppermute(give, "head", [(0, 1), (1, 0)])
    keep = project(half, attn_t, w_out, jnp.float32)
    return (keep + got.astype(jnp.float32)).astype(jnp.bfloat16)


def solution(mesh):
    placed = (
        P("seq", "head"),
        P("seq", "head"),
        P("seq", "head"),
        P("seq", "head"),
        P("seq", "head"),
        P(None, "head"),
        P(None, "head"),
        P(),
        P(),
        P("head", None),
    )
    return jax.shard_map(
        shards, mesh=mesh, in_specs=placed, out_specs=P("head", "seq"), check_vma=False
    )
```

profile of v0, /device:TPU:31, one launch (start us, length us, event | category | flops | bytes accessed | tf_op | source)
XLA Modules:
  0.0 117.2 jit_solution(13058102820553521583)
XLA Ops:
  0.0 2.4 %pack.1 = bf16[16,224,128]{2,1,0:T(8,128)(2,1)} custom-call(bf16[128,1536]{1,0:T(8,128)(2,1)} %k_ref.1, bf16[128,1536]{1,0:T(8,128)(2,1)} %v_ref.1, bf16[16,1536]{1,0:T(8,128)(2,1)} %ck_ref.1, bf16[16,1536]{1,0:T(8,128)(2,1)} %cv_ref.1), custom_call_target="tpu_custom_call" | custom-call | tf_op jit(solution)/shard_map/pack/pallas_call | solution.py:384
  2.4 9.2 %all-to-all-start.1 = ((bf16[16,224,128]{2,1,0:T(8,128)(2,1)}), bf16[16,224,128]{2,1,0:T(8,128)(2,1)S(1)}, u32[]{:S(2)}, u32[]{:S(2)}) async-start(bf16[16,224,128]{2,1,0:T(8,128)(2,1)} %pack.1), calls=%async_computation.1 | async-start | bytes 1835008 | tf_op jit(solution)/shard_map/all_to_all | solution.py:411
  11.5 0.1 pad_add_fusion.place
  11.6 1.0 copy-done
  12.6 0.7 copy-done.1
  13.3 0.7 copy-done.2
  14.1 0.7 copy-done.3
  14.7 0.7 copy-done.4
  15.4 2.4 %pack_query.1 = (bf16[16,96,128]{2,1,0:T(8,128)(2,1)}, bf16[32,128]{1,0:T(8,128)(2,1)S(1)}, s32[8,8,256]{2,1,0:T(8,128)S(1)}, s32[25]{0:T(128)S(1)}) custom-call(s32[2]{0:T(128)S(1)} %pad_add_fusion.place, s32[32]{0:T(128)S(1)} %copy-done.3, s32[32]{0:T(128)S(1)} %copy-done.4, bf16[128,1536]{1,0:T(8,128)(2,1)S(1)} %copy-done, bf16[8,1536]{1,0:T(8,128)(2,1)S(1)} %copy-done.1, ...), custom_call_target="tpu_custom_call" | custom-call | flops 1048576 | bytes 2097152 | tf_op jit(solution)/shard_map/pack_query/pallas_call | solution.py:394
  17.8 19.1 %all-to-all-done.1.own_ref = bf16[16,224,128]{2,1,0:T(8,128)(2,1)S(1)} async-done(((bf16[16,224,128]{2,1,0:T(8,128)(2,1)}), bf16[16,224,128]{2,1,0:T(8,128)(2,1)S(1)}, u32[]{:S(2)}, u32[]{:S(2)}) %all-to-all-start.1) | async-done | bytes 917536 | tf_op jit(solution)/shard_map/all_to_all | solution.py:411
  36.9 3.5 %all-to-all-start = ((bf16[16,96,128]{2,1,0:T(8,128)(2,1)}), bf16[16,96,128]{2,1,0:T(8,128)(2,1)S(1)}, u32[]{:S(2)}, u32[]{:S(2)}) async-start(bf16[16,96,128]{2,1,0:T(8,128)(2,1)} %get-tuple-element.16), calls=%async_computation | async-start | bytes 786432 | tf_op jit(solution)/shard_map/all_to_all | solution.py:411
  40.4 0.6 collective-permute-start.4
  41.0 1.0 collective-permute-start.2
  42.0 1.9 %collective-permute-start.3 = (bf16[16,32,128]{2,1,0:T(8,128)(2,1)S(1)}, bf16[16,32,128]{2,1,0:T(8,128)(2,1)S(1)}, u32[]{:S(2)}, u32[]{:S(2)}) collective-permute-start(bf16[16,32,128]{2,1,0:T(8,128)(2,1)S(1)} %slice.4.rest_0_), channel_id=1, source_target_pairs={{0,32},{2,34},{4,36},{6,38},{8,40},{10,42},{12,44},{14,46},{16,48}... | collective-permute-start | bytes 393224 | tf_op jit(solution)/shard_map/ppermute | solution.py:422
  43.9 0.2 prep.1
  44.1 1.3 %collective-permute-start = (bf16[8,192,128]{2,1,0:T(8,128)(2,1)S(1)}, bf16[8,192,128]{2,1,0:T(8,128)(2,1)S(1)}, u32[]{:S(2)}, u32[]{:S(2)}) collective-permute-start(bf16[8,192,128]{2,1,0:T(8,128)(2,1)S(1)} %get-tuple-element.17), channel_id=1, source_target_pairs={{0,32},{2,34},{4,36},{6,38},{8,40},{10,42},{12,44},{14,46},{16,48}... | collective-permute-start | bytes 1179656 | tf_op jit(solution)/shard_map/ppermute | solution.py:446
  45.4 2.2 %collective-permute-start.1 = (bf16[16,32,128]{2,1,0:T(8,128)(2,1)S(1)}, bf16[16,32,128]{2,1,0:T(8,128)(2,1)S(1)}, u32[]{:S(2)}, u32[]{:S(2)}) collective-permute-start(bf16[16,32,128]{2,1,0:T(8,128)(2,1)S(1)} %slice.4.rest_0_), channel_id=1, source_target_pairs={{0,96},{2,98},{4,100},{6,102},{8,104},{10,106},{12,108},{14,110},{... | collective-permute-start | bytes 393224 | tf_op jit(solution)/shard_map/ppermute | solution.py:422
  47.5 0.1 collective-permute-start.5
  47.6 0.9 collective-permute-start.6
  48.5 0.5 collective-permute-start.7
  49.1 5.4 %all-to-all-done.query_ref = bf16[16,96,128]{2,1,0:T(8,128)(2,1)S(1)} async-done(((bf16[16,96,128]{2,1,0:T(8,128)(2,1)}), bf16[16,96,128]{2,1,0:T(8,128)(2,1)S(1)}, u32[]{:S(2)}, u32[]{:S(2)}) %all-to-all-start) | async-done | bytes 393248 | tf_op jit(solution)/shard_map/all_to_all | solution.py:411
  54.5 4.4 %collective-permute-done.6.rest_6_ = bf16[16,32,128]{2,1,0:T(8,128)(2,1)} collective-permute-done((bf16[16,32,128]{2,1,0:T(8,128)(2,1)S(1)}, bf16[16,32,128]{2,1,0:T(8,128)(2,1)}, u32[]{:S(2)}, u32[]{:S(2)}) %collective-permute-start.6) | collective-permute-done | bytes 131104 | tf_op jit(solution)/shard_map/ppermute | solution.py:422
  58.9 2.8 %collective-permute-done.7.rest_7_ = bf16[16,32,128]{2,1,0:T(8,128)(2,1)} collective-permute-done((bf16[16,32,128]{2,1,0:T(8,128)(2,1)S(1)}, bf16[16,32,128]{2,1,0:T(8,128)(2,1)}, u32[]{:S(2)}, u32[]{:S(2)}) %collective-permute-start.7) | collective-permute-done | bytes 131104 | tf_op jit(solution)/shard_map/ppermute | solution.py:422
  61.7 13.7 %attend.1 = (bf16[8,96,128]{2,1,0:T(8,128)(2,1)S(1)}, f32[4,16,256]{2,1,0:T(8,128)S(1)}, f32[4,96,256]{2,1,0:T(8,128)S(1)}) custom-call(s32[25]{0:T(128)S(1)} %get-tuple-element.14.need, s32[8,8,256]{2,1,0:T(8,128)S(1)} %get-tuple-element.15.low_ref, bf16[32,128]{1,0:T(8,128)(2,1)S(1)} %get-tuple-element.18.sink_ref, ...), custom_call_target="tpu_custom_call" | custom-call | flops 1610612736 | bytes 4194304 | tf_op jit(solution)/shard_map/attend/pallas_call | solution.py:448
  75.4 3.4 %window.1 = bf16[16,96,128]{2,1,0:T(8,128)(2,1)} custom-call(s32[25]{0:T(128)S(1)} %get-tuple-element.14.need, s32[8,8,256]{2,1,0:T(8,128)S(1)} %get-tuple-element.15.low_ref, bf16[16,96,128]{2,1,0:T(8,128)(2,1)S(1)} %all-to-all-done.query_ref, bf16[8,192,128]{2,1,0:T(8,128)(2,1)S(1)} %collective-permute-done.win_ref, ...), custom_call_target="tpu_custom_call" | custom-call | tf_op jit(solution)/shard_map/window/pallas_call | solution.py:468
  78.8 8.2 %all-to-all-start.2 = ((bf16[16,96,128]{2,1,0:T(8,128)(2,1)}), bf16[16,96,128]{2,1,0:T(8,128)(2,1)S(1)}, u32[]{:S(2)}, u32[]{:S(2)}) async-start(bf16[16,96,128]{2,1,0:T(8,128)(2,1)} %window.1), calls=%async_computation.2 | async-start | bytes 786432 | tf_op jit(solution)/shard_map/all_to_all | solution.py:411
  87.0 14.5 %all-to-all-done.2 = bf16[16,96,128]{2,1,0:T(8,128)(2,1)S(1)} async-done(((bf16[16,96,128]{2,1,0:T(8,128)(2,1)}), bf16[16,96,128]{2,1,0:T(8,128)(2,1)S(1)}, u32[]{:S(2)}, u32[]{:S(2)}) %all-to-all-start.2) | async-done | bytes 393248 | tf_op jit(solution)/shard_map/all_to_all | solution.py:411
  101.5 2.7 %project.3 = bf16[1536,128]{1,0:T(8,128)(2,1)S(1)} custom-call(s32[1]{0:T(128)} %bitcast.4.side, bf16[1536,128]{1,0:T(8,128)(2,1)S(1)} %bitcast.5, bf16[1536,3072]{1,0:T(8,128)(2,1)} %w_ref.3), custom_call_target="tpu_custom_call" | custom-call | flops 603979776 | bytes 4718592 | tf_op jit(solution)/shard_map/project/pallas_call | solution.py:347
  104.2 0.9 collective-permute-start.8
  105.1 2.8 %project.2 = f32[1536,128]{1,0:T(8,128)S(1)} custom-call(s32[1]{0:T(128)} %bitcast.side, bf16[1536,128]{1,0:T(8,128)(2,1)S(1)} %bitcast.6, bf16[1536,3072]{1,0:T(8,128)(2,1)} %w_ref.3), custom_call_target="tpu_custom_call" | custom-call | flops 603979776 | bytes 4718592 | tf_op jit(solution)/shard_map/project/pallas_call | solution.py:347
  108.0 8.4 %collective-permute-done.8 = bf16[1536,128]{1,0:T(8,128)(2,1)S(1)} collective-permute-done((bf16[1536,128]{1,0:T(8,128)(2,1)S(1)}, bf16[1536,128]{1,0:T(8,128)(2,1)S(1)}, u32[]{:S(2)}, u32[]{:S(2)}) %collective-permute-start.8) | collective-permute-done | bytes 393248 | tf_op jit(solution)/shard_map/ppermute | solution.py:483
  116.4 0.8 add_convert_fusion
  (12 shorter events, 0.0 us)
Async XLA Ops:
  2.4 34.5 %all-to-all-start.1 = ((bf16[16,224,128]{2,1,0:T(8,128)(2,1)}), bf16[16,224,128]{2,1,0:T(8,128)(2,1)S(1)}, u32[]{:S(2)}, u32[]{:S(2)}) async-start(bf16[16,224,128]{2,1,0:T(8,128)(2,1)} %pack.1), calls=%async_computation.1 | async-start | bytes 1835008 | tf_op jit(solution)/shard_map/all_to_all | solution.py:411
  11.6 1.0 copy-start
  12.6 0.7 copy-start.1
  13.3 0.7 copy-start.2
  14.1 0.7 copy-start.3
  14.7 0.7 copy-start.4
  36.9 17.6 %all-to-all-start = ((bf16[16,96,128]{2,1,0:T(8,128)(2,1)}), bf16[16,96,128]{2,1,0:T(8,128)(2,1)S(1)}, u32[]{:S(2)}, u32[]{:S(2)}) async-start(bf16[16,96,128]{2,1,0:T(8,128)(2,1)} %get-tuple-element.16), calls=%async_computation | async-start | bytes 786432 | tf_op jit(solution)/shard_map/all_to_all | solution.py:411
  40.4 7.2 %collective-permute-start.4 = (bf16[16,32,128]{2,1,0:T(8,128)(2,1)S(1)}, bf16[16,32,128]{2,1,0:T(8,128)(2,1)S(1)}, u32[]{:S(2)}, u32[]{:S(2)}) collective-permute-start(bf16[16,32,128]{2,1,0:T(8,128)(2,1)S(1)} %slice.4.rest_0_), channel_id=1, source_target_pairs={{0,128},{2,130},{4,132},{6,134},{8,136},{10,138},{12,140},{14,142}... | collective-permute-start | bytes 393224 | tf_op jit(solution)/shard_map/ppermute | solution.py:422
  41.0 6.6 %collective-permute-start.2 = (bf16[16,32,128]{2,1,0:T(8,128)(2,1)S(1)}, bf16[16,32,128]{2,1,0:T(8,128)(2,1)S(1)}, u32[]{:S(2)}, u32[]{:S(2)}) collective-permute-start(bf16[16,32,128]{2,1,0:T(8,128)(2,1)S(1)} %slice.4.rest_0_), channel_id=1, source_target_pairs={{0,64},{2,66},{4,68},{6,70},{8,72},{10,74},{12,76},{14,78},{16,80}... | collective-permute-start | bytes 393224 | tf_op jit(solution)/shard_map/ppermute | solution.py:422
  42.0 6.6 %collective-permute-start.3 = (bf16[16,32,128]{2,1,0:T(8,128)(2,1)S(1)}, bf16[16,32,128]{2,1,0:T(8,128)(2,1)S(1)}, u32[]{:S(2)}, u32[]{:S(2)}) collective-permute-start(bf16[16,32,128]{2,1,0:T(8,128)(2,1)S(1)} %slice.4.rest_0_), channel_id=1, source_target_pairs={{0,32},{2,34},{4,36},{6,38},{8,40},{10,42},{12,44},{14,46},{16,48}... | collective-permute-start | bytes 393224 | tf_op jit(solution)/shard_map/ppermute | solution.py:422
  44.1 31.3 %collective-permute-start = (bf16[8,192,128]{2,1,0:T(8,128)(2,1)S(1)}, bf16[8,192,128]{2,1,0:T(8,128)(2,1)S(1)}, u32[]{:S(2)}, u32[]{:S(2)}) collective-permute-start(bf16[8,192,128]{2,1,0:T(8,128)(2,1)S(1)} %get-tuple-element.17), channel_id=1, source_target_pairs={{0,32},{2,34},{4,36},{6,38},{8,40},{10,42},{12,44},{14,46},{16,48}... | collective-permute-start | bytes 1179656 | tf_op jit(solution)/shard_map/ppermute | solution.py:446
  45.4 9.2 %collective-permute-start.1 = (bf16[16,32,128]{2,1,0:T(8,128)(2,1)S(1)}, bf16[16,32,128]{2,1,0:T(8,128)(2,1)S(1)}, u32[]{:S(2)}, u32[]{:S(2)}) collective-permute-start(bf16[16,32,128]{2,1,0:T(8,128)(2,1)S(1)} %slice.4.rest_0_), channel_id=1, source_target_pairs={{0,96},{2,98},{4,100},{6,102},{8,104},{10,106},{12,108},{14,110},{... | collective-permute-start | bytes 393224 | tf_op jit(solution)/shard_map/ppermute | solution.py:422
  47.5 7.0 %collective-permute-start.5 = (bf16[16,32,128]{2,1,0:T(8,128)(2,1)S(1)}, bf16[16,32,128]{2,1,0:T(8,128)(2,1)S(1)}, u32[]{:S(2)}, u32[]{:S(2)}) collective-permute-start(bf16[16,32,128]{2,1,0:T(8,128)(2,1)S(1)} %collective-permute-done.4.rest_4_), channel_id=1, source_target_pairs={{0,96},{2,98},{4,100},{6,102},{8,104},{10,106},{12,108},{14,110},{... | collective-permute-start | bytes 393224 | tf_op jit(solution)/shard_map/ppermute | solution.py:422
  47.6 11.3 %collective-permute-start.6 = (bf16[16,32,128]{2,1,0:T(8,128)(2,1)S(1)}, bf16[16,32,128]{2,1,0:T(8,128)(2,1)}, u32[]{:S(2)}, u32[]{:S(2)}) collective-permute-start(bf16[16,32,128]{2,1,0:T(8,128)(2,1)S(1)} %collective-permute-done.2.rest_2_), channel_id=1, source_target_pairs={{0,128},{2,130},{4,132},{6,134},{8,136},{10,138},{12,140},{14,142}... | collective-permute-start | bytes 393224 | tf_op jit(solution)/shard_map/ppermute | solution.py:422
  48.5 13.2 %collective-permute-start.7 = (bf16[16,32,128]{2,1,0:T(8,128)(2,1)S(1)}, bf16[16,32,128]{2,1,0:T(8,128)(2,1)}, u32[]{:S(2)}, u32[]{:S(2)}) collective-permute-start(bf16[16,32,128]{2,1,0:T(8,128)(2,1)S(1)} %collective-permute-done.3.rest_3_), channel_id=1, source_target_pairs={{0,128},{2,130},{4,132},{6,134},{8,136},{10,138},{12,140},{14,142}... | collective-permute-start | bytes 393224 | tf_op jit(solution)/shard_map/ppermute | solution.py:422
  78.8 22.7 %all-to-all-start.2 = ((bf16[16,96,128]{2,1,0:T(8,128)(2,1)}), bf16[16,96,128]{2,1,0:T(8,128)(2,1)S(1)}, u32[]{:S(2)}, u32[]{:S(2)}) async-start(bf16[16,96,128]{2,1,0:T(8,128)(2,1)} %window.1), calls=%async_computation.2 | async-start | bytes 786432 | tf_op jit(solution)/shard_map/all_to_all | solution.py:411
  104.2 12.1 %collective-permute-start.8 = (bf16[1536,128]{1,0:T(8,128)(2,1)S(1)}, bf16[1536,128]{1,0:T(8,128)(2,1)S(1)}, u32[]{:S(2)}, u32[]{:S(2)}) collective-permute-start(bf16[1536,128]{1,0:T(8,128)(2,1)S(1)} %project.3), channel_id=1, source_target_pairs={{0,1},{1,0},{2,3},{3,2},{4,5},{5,4},{6,7},{7,6},{8,9},{9,8},{10,11... | collective-permute-start | bytes 1179656 | tf_op jit(solution)/shard_map/ppermute | solution.py:483
where the time goes:
time: 118 us; the launch traced here: 117 us
  waiting for transfers between devices  54.6 us (46%)
  starting transfers between devices  30.3 us (26%)
  Pallas kernels  27.5 us (23%)
  local copies, waits for them, and re-layouts  3.79 us (3%)
    all_to_all x3, waiting for transfers between devices, trade(): lax.all_to_all(array, 'seq', 0, 0, axis_index_groups=groups, tiled=True)  39.1 us
    all_to_all x3, starting transfers between devices, trade(): lax.all_to_all(array, 'seq', 0, 0, axis_index_groups=groups, tiled=True)  20.8 us
    pallas_call x1, Pallas kernels, shards(): pl.pallas_call(functools.partial(attend_kernel, rings=rings), out_shape=(...  13.7 us
    ppermute x1, waiting for transfers between devices, shards(): got = lax.ppermute(give, 'head', [(0, 1), (1, 0)])  8.38 us
    ppermute x7, starting transfers between devices, send(): return lax.ppermute(array, 'seq', pairs)  7.22 us
    ppermute x7, waiting for transfers between devices, send(): return lax.ppermute(array, 'seq', pairs)  7.19 us
    pallas_call x2, Pallas kernels, project(): pl.pallas_call(project_kernel, out_shape=jax.ShapeDtypeStruct((features,...  5.54 us
    unnamed x10, local copies, waits for them, and re-layouts  3.78 us
  transfers between devices with their start and end apart: 12, of which 6 were waited for; matrix products, arithmetic and copies ran while one was open for 0% of the time, Pallas kernels for 16%

commit v1 on v0

--- a/solution.py
+++ b/solution.py
@@ -193,6 +193,33 @@
     return top, den, acc + dot(values(val_ref, before), p_odd[...])
 
 
+def visit_plain(total, where_is, key_ref, val_ref, low_of, q_t, state):
+    row_iota = lax.broadcasted_iota(jnp.int32, (CH, QB), 0)
+
+    def step(j, state):
+        top, den, acc = state
+        scores, ats = [], []
+        for u in range(2):
+            at, kind = where_is(2 * j + u)
+            s = dot(key_ref[pl.ds(at, CH), :], q_t)
+            scores.append(jnp.where(row_iota >= low_of(kind) - at, s, LOW))
+            ats.append(at)
+        peak = jnp.maximum(fold(scores[0], jnp.max), fold(scores[1], jnp.max))
+        new = jnp.maximum(top, jnp.max(peak, axis=0, keepdims=True))
+        fade = jnp.exp2((top - new) * FACTOR)
+        den = den * fade
+        ps = []
+        for u in range(2):
+            p = jnp.exp2((scores[u] - new) * FACTOR)
+            den = den + fold(p, jnp.sum)
+            ps.append(p.astype(jnp.bfloat16))
+        vals = jnp.concatenate([values(val_ref, at) for at in ats], axis=1)
+        acc = acc * fade + dot(vals, jnp.concatenate(ps, axis=0))
+        return (new, den, acc)
+
+    return lax.fori_loop(0, (total + 1) // 2, step, state)
+
+
 def attend_kernel(
     need, low_ref, sink_ref, query_ref, own_ref, turned_ref, *rest, rings
 ):
@@ -282,7 +309,7 @@
 
 def window_kernel(
     need, low_ref, query_ref, win_ref, upper_ref, stat_ref, acc_ref, out_ref,
-    key_ref, val_ref, *buffers,
+    key_ref, val_ref,
 ):
     blocks = RING * BLK // QB
     base = need[(1 + G) * blocks] * RING * BLK
@@ -304,9 +331,8 @@
         def low_of(kind):
             return low_ref[b, pl.ds(kind, 1), :] + jnp.where(kind == 0, W, 0)
 
-        buffers[3][...] = jnp.zeros((CH, QB), jnp.bfloat16)
-        state = (stat_ref[b, 0:1, :], stat_ref[b, 8:16, :], acc_ref[b], jnp.int32(0))
-        _, den, acc = visit(total, where_is, key_ref, val_ref, low_of, q_t, state, buffers)
+        state = (stat_ref[b, 0:1, :], stat_ref[b, 8:16, :], acc_ref[b])
+        _, den, acc = visit_plain(total, where_is, key_ref, val_ref, low_of, q_t, state)
         done = (acc / jnp.sum(den, axis=0, keepdims=True)).astype(jnp.bfloat16)
         out_ref[2 * b] = done[:, 0:BLK]
         out_ref[2 * b + 1] = done[:, BLK:QB]
@@ -473,7 +499,6 @@
         scratch_shapes=[
             pltpu.VMEM((W, LANES), jnp.bfloat16),
             pltpu.VMEM((W // BLK, HD, BLK), jnp.bfloat16),
-            *buffers,
         ],
         compiler_params=pltpu.CompilerParams(vmem_limit_bytes=VMEM_LIMIT),
         name="window",

time: 118 us -> 117 us (level)
  no operation moved by 1% of the time
where the time goes in v1:
time: 117 us; the launch traced here: 116 us
  waiting for transfers between devices  54.6 us (47%)
  starting transfers between devices  30.3 us (26%)
  Pallas kernels  26.6 us (23%)
  local copies, waits for them, and re-layouts  3.79 us (3%)
    all_to_all x3, waiting for transfers between devices, trade(): lax.all_to_all(array, 'seq', 0, 0, axis_index_groups=groups, tiled=True)  39.1 us
    all_to_all x3, starting transfers between devices, trade(): lax.all_to_all(array, 'seq', 0, 0, axis_index_groups=groups, tiled=True)  20.8 us
    pallas_call x1, Pallas kernels, shards(): pl.pallas_call(functools.partial(attend_kernel, rings=rings), out_shape=(...  13.7 us
    ppermute x1, waiting for transfers between devices, shards(): got = lax.ppermute(give, 'head', [(0, 1), (1, 0)])  8.38 us
    ppermute x7, starting transfers between devices, send(): return lax.ppermute(array, 'seq', pairs)  7.22 us
    ppermute x7, waiting for transfers between devices, send(): return lax.ppermute(array, 'seq', pairs)  7.19 us
    pallas_call x2, Pallas kernels, project(): pl.pallas_call(project_kernel, out_shape=jax.ShapeDtypeStruct((features,...  5.54 us
    unnamed x10, local copies, waits for them, and re-layouts  3.78 us
  transfers between devices with their start and end apart: 12, of which 6 were waited for; matrix products, arithmetic and copies ran while one was open for 0% of the time, Pallas kernels for 16%

profile of v1, /device:TPU:31, one launch (start us, length us, event | category | flops | bytes accessed | tf_op | source)
XLA Modules:
  0.0 116.3 jit_solution(13736259975910734990)
XLA Ops:
  0.0 2.4 %pack.1 = bf16[16,224,128]{2,1,0:T(8,128)(2,1)} custom-call(bf16[128,1536]{1,0:T(8,128)(2,1)} %k_ref.1, bf16[128,1536]{1,0:T(8,128)(2,1)} %v_ref.1, bf16[16,1536]{1,0:T(8,128)(2,1)} %ck_ref.1, bf16[16,1536]{1,0:T(8,128)(2,1)} %cv_ref.1), custom_call_target="tpu_custom_call" | custom-call | tf_op jit(solution)/shard_map/pack/pallas_call | solution.py:410
  2.4 9.2 %all-to-all-start.1 = ((bf16[16,224,128]{2,1,0:T(8,128)(2,1)}), bf16[16,224,128]{2,1,0:T(8,128)(2,1)S(1)}, u32[]{:S(2)}, u32[]{:S(2)}) async-start(bf16[16,224,128]{2,1,0:T(8,128)(2,1)} %pack.1), calls=%async_computation.1 | async-start | bytes 1835008 | tf_op jit(solution)/shard_map/all_to_all | solution.py:437
  11.5 0.1 pad_add_fusion.place
  11.6 1.0 copy-done
  12.6 0.7 copy-done.1
  13.3 0.7 copy-done.2
  14.1 0.7 copy-done.3
  14.7 0.7 copy-done.4
  15.4 2.4 %pack_query.1 = (bf16[16,96,128]{2,1,0:T(8,128)(2,1)}, bf16[32,128]{1,0:T(8,128)(2,1)S(1)}, s32[8,8,256]{2,1,0:T(8,128)S(1)}, s32[25]{0:T(128)S(1)}) custom-call(s32[2]{0:T(128)S(1)} %pad_add_fusion.place, s32[32]{0:T(128)S(1)} %copy-done.3, s32[32]{0:T(128)S(1)} %copy-done.4, bf16[128,1536]{1,0:T(8,128)(2,1)S(1)} %copy-done, bf16[8,1536]{1,0:T(8,128)(2,1)S(1)} %copy-done.1, ...), custom_call_target="tpu_custom_call" | custom-call | flops 1048576 | bytes 2097152 | tf_op jit(solution)/shard_map/pack_query/pallas_call | solution.py:420
  17.8 19.1 %all-to-all-done.1.own_ref = bf16[16,224,128]{2,1,0:T(8,128)(2,1)S(1)} async-done(((bf16[16,224,128]{2,1,0:T(8,128)(2,1)}), bf16[16,224,128]{2,1,0:T(8,128)(2,1)S(1)}, u32[]{:S(2)}, u32[]{:S(2)}) %all-to-all-start.1) | async-done | bytes 917536 | tf_op jit(solution)/shard_map/all_to_all | solution.py:437
  36.9 3.5 %all-to-all-start = ((bf16[16,96,128]{2,1,0:T(8,128)(2,1)}), bf16[16,96,128]{2,1,0:T(8,128)(2,1)S(1)}, u32[]{:S(2)}, u32[]{:S(2)}) async-start(bf16[16,96,128]{2,1,0:T(8,128)(2,1)} %get-tuple-element.16), calls=%async_computation | async-start | bytes 786432 | tf_op jit(solution)/shard_map/all_to_all | solution.py:437
  40.4 0.6 collective-permute-start.4
  41.0 1.0 collective-permute-start.2
  42.0 1.9 %collective-permute-start.3 = (bf16[16,32,128]{2,1,0:T(8,128)(2,1)S(1)}, bf16[16,32,128]{2,1,0:T(8,128)(2,1)S(1)}, u32[]{:S(2)}, u32[]{:S(2)}) collective-permute-start(bf16[16,32,128]{2,1,0:T(8,128)(2,1)S(1)} %slice.4.rest_0_), channel_id=1, source_target_pairs={{0,32},{2,34},{4,36},{6,38},{8,40},{10,42},{12,44},{14,46},{16,48}... | collective-permute-start | bytes 393224 | tf_op jit(solution)/shard_map/ppermute | solution.py:448
  43.9 0.2 prep.1
  44.1 1.3 %collective-permute-start = (bf16[8,192,128]{2,1,0:T(8,128)(2,1)S(1)}, bf16[8,192,128]{2,1,0:T(8,128)(2,1)S(1)}, u32[]{:S(2)}, u32[]{:S(2)}) collective-permute-start(bf16[8,192,128]{2,1,0:T(8,128)(2,1)S(1)} %get-tuple-element.17), channel_id=1, source_target_pairs={{0,32},{2,34},{4,36},{6,38},{8,40},{10,42},{12,44},{14,46},{16,48}... | collective-permute-start | bytes 1179656 | tf_op jit(solution)/shard_map/ppermute | solution.py:472
  45.4 2.2 %collective-permute-start.1 = (bf16[16,32,128]{2,1,0:T(8,128)(2,1)S(1)}, bf16[16,32,128]{2,1,0:T(8,128)(2,1)S(1)}, u32[]{:S(2)}, u32[]{:S(2)}) collective-permute-start(bf16[16,32,128]{2,1,0:T(8,128)(2,1)S(1)} %slice.4.rest_0_), channel_id=1, source_target_pairs={{0,96},{2,98},{4,100},{6,102},{8,104},{10,106},{12,108},{14,110},{... | collective-permute-start | bytes 393224 | tf_op jit(solution)/shard_map/ppermute | solution.py:448
  47.5 0.1 collective-permute-start.5
  47.6 0.9 collective-permute-start.6
  48.5 0.5 collective-permute-start.7
  49.1 5.4 %all-to-all-done.query_ref = bf16[16,96,128]{2,1,0:T(8,128)(2,1)S(1)} async-done(((bf16[16,96,128]{2,1,0:T(8,128)(2,1)}), bf16[16,96,128]{2,1,0:T(8,128)(2,1)S(1)}, u32[]{:S(2)}, u32[]{:S(2)}) %all-to-all-start) | async-done | bytes 393248 | tf_op jit(solution)/shard_map/all_to_all | solution.py:437
  54.5 4.4 %collective-permute-done.6.rest_6_ = bf16[16,32,128]{2,1,0:T(8,128)(2,1)} collective-permute-done((bf16[16,32,128]{2,1,0:T(8,128)(2,1)S(1)}, bf16[16,32,128]{2,1,0:T(8,128)(2,1)}, u32[]{:S(2)}, u32[]{:S(2)}) %collective-permute-start.6) | collective-permute-done | bytes 131104 | tf_op jit(solution)/shard_map/ppermute | solution.py:448
  58.9 2.8 %collective-permute-done.7.rest_7_ = bf16[16,32,128]{2,1,0:T(8,128)(2,1)} collective-permute-done((bf16[16,32,128]{2,1,0:T(8,128)(2,1)S(1)}, bf16[16,32,128]{2,1,0:T(8,128)(2,1)}, u32[]{:S(2)}, u32[]{:S(2)}) %collective-permute-start.7) | collective-permute-done | bytes 131104 | tf_op jit(solution)/shard_map/ppermute | solution.py:448
  61.7 13.7 %attend.1 = (bf16[8,96,128]{2,1,0:T(8,128)(2,1)S(1)}, f32[4,16,256]{2,1,0:T(8,128)S(1)}, f32[4,96,256]{2,1,0:T(8,128)S(1)}) custom-call(s32[25]{0:T(128)S(1)} %get-tuple-element.14.need, s32[8,8,256]{2,1,0:T(8,128)S(1)} %get-tuple-element.15.low_ref, bf16[32,128]{1,0:T(8,128)(2,1)S(1)} %get-tuple-element.18.sink_ref, ...), custom_call_target="tpu_custom_call" | custom-call | flops 1610612736 | bytes 4194304 | tf_op jit(solution)/shard_map/attend/pallas_call | solution.py:474
  75.4 2.5 %window.1 = bf16[16,96,128]{2,1,0:T(8,128)(2,1)} custom-call(s32[25]{0:T(128)S(1)} %get-tuple-element.14.need, s32[8,8,256]{2,1,0:T(8,128)S(1)} %get-tuple-element.15.low_ref, bf16[16,96,128]{2,1,0:T(8,128)(2,1)S(1)} %all-to-all-done.query_ref, bf16[8,192,128]{2,1,0:T(8,128)(2,1)S(1)} %collective-permute-done.win_ref, ...), custom_call_target="tpu_custom_call" | custom-call | tf_op jit(solution)/shard_map/window/pallas_call | solution.py:494
  77.9 8.2 %all-to-all-start.2 = ((bf16[16,96,128]{2,1,0:T(8,128)(2,1)}), bf16[16,96,128]{2,1,0:T(8,128)(2,1)S(1)}, u32[]{:S(2)}, u32[]{:S(2)}) async-start(bf16[16,96,128]{2,1,0:T(8,128)(2,1)} %window.1), calls=%async_computation.2 | async-start | bytes 786432 | tf_op jit(solution)/shard_map/all_to_all | solution.py:437
  86.1 14.5 %all-to-all-done.2 = bf16[16,96,128]{2,1,0:T(8,128)(2,1)S(1)} async-done(((bf16[16,96,128]{2,1,0:T(8,128)(2,1)}), bf16[16,96,128]{2,1,0:T(8,128)(2,1)S(1)}, u32[]{:S(2)}, u32[]{:S(2)}) %all-to-all-start.2) | async-done | bytes 393248 | tf_op jit(solution)/shard_map/all_to_all | solution.py:437
  100.6 2.7 %project.3 = bf16[1536,128]{1,0:T(8,128)(2,1)S(1)} custom-call(s32[1]{0:T(128)} %bitcast.4.side, bf16[1536,128]{1,0:T(8,128)(2,1)S(1)} %bitcast.5, bf16[1536,3072]{1,0:T(8,128)(2,1)} %w_ref.3), custom_call_target="tpu_custom_call" | custom-call | flops 603979776 | bytes 4718592 | tf_op jit(solution)/shard_map/project/pallas_call | solution.py:373
  103.4 0.9 collective-permute-start.8
  104.3 2.8 %project.2 = f32[1536,128]{1,0:T(8,128)S(1)} custom-call(s32[1]{0:T(128)} %bitcast.side, bf16[1536,128]{1,0:T(8,128)(2,1)S(1)} %bitcast.6, bf16[1536,3072]{1,0:T(8,128)(2,1)} %w_ref.3), custom_call_target="tpu_custom_call" | custom-call | flops 603979776 | bytes 4718592 | tf_op jit(solution)/shard_map/project/pallas_call | solution.py:373
  107.1 8.4 %collective-permute-done.8 = bf16[1536,128]{1,0:T(8,128)(2,1)S(1)} collective-permute-done((bf16[1536,128]{1,0:T(8,128)(2,1)S(1)}, bf16[1536,128]{1,0:T(8,128)(2,1)S(1)}, u32[]{:S(2)}, u32[]{:S(2)}) %collective-permute-start.8) | collective-permute-done | bytes 393248 | tf_op jit(solution)/shard_map/ppermute | solution.py:508
  115.5 0.8 add_convert_fusion
  (12 shorter events, 0.0 us)
Async XLA Ops:
  2.4 34.5 %all-to-all-start.1 = ((bf16[16,224,128]{2,1,0:T(8,128)(2,1)}), bf16[16,224,128]{2,1,0:T(8,128)(2,1)S(1)}, u32[]{:S(2)}, u32[]{:S(2)}) async-start(bf16[16,224,128]{2,1,0:T(8,128)(2,1)} %pack.1), calls=%async_computation.1 | async-start | bytes 1835008 | tf_op jit(solution)/shard_map/all_to_all | solution.py:437
  11.6 1.0 copy-start
  12.6 0.7 copy-start.1
  13.3 0.7 copy-start.2
  14.1 0.7 copy-start.3
  14.7 0.7 copy-start.4
  36.9 17.6 %all-to-all-start = ((bf16[16,96,128]{2,1,0:T(8,128)(2,1)}), bf16[16,96,128]{2,1,0:T(8,128)(2,1)S(1)}, u32[]{:S(2)}, u32[]{:S(2)}) async-start(bf16[16,96,128]{2,1,0:T(8,128)(2,1)} %get-tuple-element.16), calls=%async_computation | async-start | bytes 786432 | tf_op jit(solution)/shard_map/all_to_all | solution.py:437
  40.4 7.2 %collective-permute-start.4 = (bf16[16,32,128]{2,1,0:T(8,128)(2,1)S(1)}, bf16[16,32,128]{2,1,0:T(8,128)(2,1)S(1)}, u32[]{:S(2)}, u32[]{:S(2)}) collective-permute-start(bf16[16,32,128]{2,1,0:T(8,128)(2,1)S(1)} %slice.4.rest_0_), channel_id=1, source_target_pairs={{0,128},{2,130},{4,132},{6,134},{8,136},{10,138},{12,140},{14,142}... | collective-permute-start | bytes 393224 | tf_op jit(solution)/shard_map/ppermute | solution.py:448
  41.0 6.6 %collective-permute-start.2 = (bf16[16,32,128]{2,1,0:T(8,128)(2,1)S(1)}, bf16[16,32,128]{2,1,0:T(8,128)(2,1)S(1)}, u32[]{:S(2)}, u32[]{:S(2)}) collective-permute-start(bf16[16,32,128]{2,1,0:T(8,128)(2,1)S(1)} %slice.4.rest_0_), channel_id=1, source_target_pairs={{0,64},{2,66},{4,68},{6,70},{8,72},{10,74},{12,76},{14,78},{16,80}... | collective-permute-start | bytes 393224 | tf_op jit(solution)/shard_map/ppermute | solution.py:448
  42.0 6.6 %collective-permute-start.3 = (bf16[16,32,128]{2,1,0:T(8,128)(2,1)S(1)}, bf16[16,32,128]{2,1,0:T(8,128)(2,1)S(1)}, u32[]{:S(2)}, u32[]{:S(2)}) collective-permute-start(bf16[16,32,128]{2,1,0:T(8,128)(2,1)S(1)} %slice.4.rest_0_), channel_id=1, source_target_pairs={{0,32},{2,34},{4,36},{6,38},{8,40},{10,42},{12,44},{14,46},{16,48}... | collective-permute-start | bytes 393224 | tf_op jit(solution)/shard_map/ppermute | solution.py:448
  44.1 31.3 %collective-permute-start = (bf16[8,192,128]{2,1,0:T(8,128)(2,1)S(1)}, bf16[8,192,128]{2,1,0:T(8,128)(2,1)S(1)}, u32[]{:S(2)}, u32[]{:S(2)}) collective-permute-start(bf16[8,192,128]{2,1,0:T(8,128)(2,1)S(1)} %get-tuple-element.17), channel_id=1, source_target_pairs={{0,32},{2,34},{4,36},{6,38},{8,40},{10,42},{12,44},{14,46},{16,48}... | collective-permute-start | bytes 1179656 | tf_op jit(solution)/shard_map/ppermute | solution.py:472
  45.4 9.2 %collective-permute-start.1 = (bf16[16,32,128]{2,1,0:T(8,128)(2,1)S(1)}, bf16[16,32,128]{2,1,0:T(8,128)(2,1)S(1)}, u32[]{:S(2)}, u32[]{:S(2)}) collective-permute-start(bf16[16,32,128]{2,1,0:T(8,128)(2,1)S(1)} %slice.4.rest_0_), channel_id=1, source_target_pairs={{0,96},{2,98},{4,100},{6,102},{8,104},{10,106},{12,108},{14,110},{... | collective-permute-start | bytes 393224 | tf_op jit(solution)/shard_map/ppermute | solution.py:448
  47.5 7.0 %collective-permute-start.5 = (bf16[16,32,128]{2,1,0:T(8,128)(2,1)S(1)}, bf16[16,32,128]{2,1,0:T(8,128)(2,1)S(1)}, u32[]{:S(2)}, u32[]{:S(2)}) collective-permute-start(bf16[16,32,128]{2,1,0:T(8,128)(2,1)S(1)} %collective-permute-done.4.rest_4_), channel_id=1, source_target_pairs={{0,96},{2,98},{4,100},{6,102},{8,104},{10,106},{12,108},{14,110},{... | collective-permute-start | bytes 393224 | tf_op jit(solution)/shard_map/ppermute | solution.py:448
  47.6 11.3 %collective-permute-start.6 = (bf16[16,32,128]{2,1,0:T(8,128)(2,1)S(1)}, bf16[16,32,128]{2,1,0:T(8,128)(2,1)}, u32[]{:S(2)}, u32[]{:S(2)}) collective-permute-start(bf16[16,32,128]{2,1,0:T(8,128)(2,1)S(1)} %collective-permute-done.2.rest_2_), channel_id=1, source_target_pairs={{0,128},{2,130},{4,132},{6,134},{8,136},{10,138},{12,140},{14,142}... | collective-permute-start | bytes 393224 | tf_op jit(solution)/shard_map/ppermute | solution.py:448
  48.5 13.2 %collective-permute-start.7 = (bf16[16,32,128]{2,1,0:T(8,128)(2,1)S(1)}, bf16[16,32,128]{2,1,0:T(8,128)(2,1)}, u32[]{:S(2)}, u32[]{:S(2)}) collective-permute-start(bf16[16,32,128]{2,1,0:T(8,128)(2,1)S(1)} %collective-permute-done.3.rest_3_), channel_id=1, source_target_pairs={{0,128},{2,130},{4,132},{6,134},{8,136},{10,138},{12,140},{14,142}... | collective-permute-start | bytes 393224 | tf_op jit(solution)/shard_map/ppermute | solution.py:448
  77.9 22.7 %all-to-all-start.2 = ((bf16[16,96,128]{2,1,0:T(8,128)(2,1)}), bf16[16,96,128]{2,1,0:T(8,128)(2,1)S(1)}, u32[]{:S(2)}, u32[]{:S(2)}) async-start(bf16[16,96,128]{2,1,0:T(8,128)(2,1)} %window.1), calls=%async_computation.2 | async-start | bytes 786432 | tf_op jit(solution)/shard_map/all_to_all | solution.py:437
  103.4 12.1 %collective-permute-start.8 = (bf16[1536,128]{1,0:T(8,128)(2,1)S(1)}, bf16[1536,128]{1,0:T(8,128)(2,1)S(1)}, u32[]{:S(2)}, u32[]{:S(2)}) collective-permute-start(bf16[1536,128]{1,0:T(8,128)(2,1)S(1)} %project.3), channel_id=1, source_target_pairs={{0,1},{1,0},{2,3},{3,2},{4,5},{5,4},{6,7},{7,6},{8,9},{9,8},{10,11... | collective-permute-start | bytes 1179656 | tf_op jit(solution)/shard_map/ppermute | solution.py:508

commit v2 on v1

--- a/solution.py
+++ b/solution.py
@@ -247,7 +247,7 @@
     sink_row = lax.broadcasted_iota(jnp.int32, (16, QB), 0)
     sink_v = sink_ref[16:32, :].T[0:HD, :]
 
-    def one_block(b, _):
+    def one_block(b):
         low_suffix = low_ref[b, 0:1, :]
         group_q = low_ref[b, 2 + G : 3 + G, :]
         q_t = query_block(query_ref, b)
@@ -304,7 +304,8 @@
 
         return 0
 
-    lax.fori_loop(0, blocks, one_block, 0)
+    for b in range(blocks):
+        one_block(b)
 
 
 def window_kernel(
@@ -318,7 +319,7 @@
         val_ref[j] = win_ref[j, HD : 2 * HD, :]
         out_ref[RING // 2 + j] = upper_ref[j]
 
-    def one_block(b, _):
+    def one_block(b):
         q_t = query_block(query_ref, b)
         first = jnp.maximum(need[b] - base, b * QB - (W - 1)) + W
         first = jnp.minimum(first // CH, W // CH)
@@ -338,7 +339,8 @@
         out_ref[2 * b + 1] = done[:, BLK:QB]
         return 0
 
-    lax.fori_loop(0, blocks // 2, one_block, 0)
+    for b in range(blocks // 2):
+        one_block(b)
 
 
 def project_kernel(side, attn_ref, w_ref, out_ref, half_ref, sum_ref, arrived):

time: 117 us -> 115 us (0.983)
  Pallas kernels: 26.6 us -> 24.9 us
    pallas_call x1, Pallas kernels: 13.7 us -> 12 us  [shards(): pl.pallas_call(functools.partial(attend_kernel, rings=rings), out_shape=(...]
  transfers between devices with their start and end apart: 12 -> 12, of which waited for: 6 -> 6; matrix products, arithmetic and copies ran while one was open for 0% -> 0% of each run, Pallas kernels for 16% -> 15%
where the time goes in v2:
time: 115 us
  waiting for transfers between devices  54.6 us (47%)
  starting transfers between devices  30.3 us (26%)
  Pallas kernels  24.9 us (22%)
  local copies, waits for them, and re-layouts  3.79 us (3%)
    all_to_all x3, waiting for transfers between devices, trade(): lax.all_to_all(array, 'seq', 0, 0, axis_index_groups=groups, tiled=True)  39.1 us
    all_to_all x3, starting transfers between devices, trade(): lax.all_to_all(array, 'seq', 0, 0, axis_index_groups=groups, tiled=True)  20.8 us
    pallas_call x1, Pallas kernels, shards(): pl.pallas_call(functools.partial(attend_kernel, rings=rings), out_shape=(...  12 us
    ppermute x1, waiting for transfers between devices, shards(): got = lax.ppermute(give, 'head', [(0, 1), (1, 0)])  8.38 us
    ppermute x7, starting transfers between devices, send(): return lax.ppermute(array, 'seq', pairs)  7.22 us
    ppermute x7, waiting for transfers between devices, send(): return lax.ppermute(array, 'seq', pairs)  7.19 us
    pallas_call x2, Pallas kernels, project(): pl.pallas_call(project_kernel, out_shape=jax.ShapeDtypeStruct((features,...  5.54 us
    unnamed x10, local copies, waits for them, and re-layouts  3.78 us
  transfers between devices with their start and end apart: 12, of which 6 were waited for; matrix products, arithmetic and copies ran while one was open for 0% of the time, Pallas kernels for 15%

profile of v2, /device:TPU:31, one launch (start us, length us, event | category | flops | bytes accessed | tf_op | source)
XLA Modules:
  0.0 114.6 jit_solution(9532566515347301904)
XLA Ops:
  0.0 2.4 %pack.1 = bf16[16,224,128]{2,1,0:T(8,128)(2,1)} custom-call(bf16[128,1536]{1,0:T(8,128)(2,1)} %k_ref.1, bf16[128,1536]{1,0:T(8,128)(2,1)} %v_ref.1, bf16[16,1536]{1,0:T(8,128)(2,1)} %ck_ref.1, bf16[16,1536]{1,0:T(8,128)(2,1)} %cv_ref.1), custom_call_target="tpu_custom_call" | custom-call | tf_op jit(solution)/shard_map/pack/pallas_call | solution.py:412
  2.4 9.2 %all-to-all-start.1 = ((bf16[16,224,128]{2,1,0:T(8,128)(2,1)}), bf16[16,224,128]{2,1,0:T(8,128)(2,1)S(1)}, u32[]{:S(2)}, u32[]{:S(2)}) async-start(bf16[16,224,128]{2,1,0:T(8,128)(2,1)} %pack.1), calls=%async_computation.1 | async-start | bytes 1835008 | tf_op jit(solution)/shard_map/all_to_all | solution.py:439
  11.5 0.1 pad_add_fusion.place
  11.6 1.0 copy-done
  12.6 0.7 copy-done.1
  13.3 0.7 copy-done.2
  14.1 0.7 copy-done.3
  14.7 0.7 copy-done.4
  15.4 2.4 %pack_query.1 = (bf16[16,96,128]{2,1,0:T(8,128)(2,1)}, bf16[32,128]{1,0:T(8,128)(2,1)S(1)}, s32[8,8,256]{2,1,0:T(8,128)S(1)}, s32[25]{0:T(128)S(1)}) custom-call(s32[2]{0:T(128)S(1)} %pad_add_fusion.place, s32[32]{0:T(128)S(1)} %copy-done.3, s32[32]{0:T(128)S(1)} %copy-done.4, bf16[128,1536]{1,0:T(8,128)(2,1)S(1)} %copy-done, bf16[8,1536]{1,0:T(8,128)(2,1)S(1)} %copy-done.1, ...), custom_call_target="tpu_custom_call" | custom-call | flops 1048576 | bytes 2097152 | tf_op jit(solution)/shard_map/pack_query/pallas_call | solution.py:422
  17.8 19.1 %all-to-all-done.1.own_ref = bf16[16,224,128]{2,1,0:T(8,128)(2,1)S(1)} async-done(((bf16[16,224,128]{2,1,0:T(8,128)(2,1)}), bf16[16,224,128]{2,1,0:T(8,128)(2,1)S(1)}, u32[]{:S(2)}, u32[]{:S(2)}) %all-to-all-start.1) | async-done | bytes 917536 | tf_op jit(solution)/shard_map/all_to_all | solution.py:439
  36.9 3.5 %all-to-all-start = ((bf16[16,96,128]{2,1,0:T(8,128)(2,1)}), bf16[16,96,128]{2,1,0:T(8,128)(2,1)S(1)}, u32[]{:S(2)}, u32[]{:S(2)}) async-start(bf16[16,96,128]{2,1,0:T(8,128)(2,1)} %get-tuple-element.16), calls=%async_computation | async-start | bytes 786432 | tf_op jit(solution)/shard_map/all_to_all | solution.py:439
  40.4 0.6 collective-permute-start.4
  41.0 1.0 collective-permute-start.2
  42.0 1.9 %collective-permute-start.3 = (bf16[16,32,128]{2,1,0:T(8,128)(2,1)S(1)}, bf16[16,32,128]{2,1,0:T(8,128)(2,1)S(1)}, u32[]{:S(2)}, u32[]{:S(2)}) collective-permute-start(bf16[16,32,128]{2,1,0:T(8,128)(2,1)S(1)} %slice.4.rest_0_), channel_id=1, source_target_pairs={{0,32},{2,34},{4,36},{6,38},{8,40},{10,42},{12,44},{14,46},{16,48}... | collective-permute-start | bytes 393224 | tf_op jit(solution)/shard_map/ppermute | solution.py:450
  43.9 0.2 prep.1
  44.1 1.3 %collective-permute-start = (bf16[8,192,128]{2,1,0:T(8,128)(2,1)S(1)}, bf16[8,192,128]{2,1,0:T(8,128)(2,1)S(1)}, u32[]{:S(2)}, u32[]{:S(2)}) collective-permute-start(bf16[8,192,128]{2,1,0:T(8,128)(2,1)S(1)} %get-tuple-element.17), channel_id=1, source_target_pairs={{0,32},{2,34},{4,36},{6,38},{8,40},{10,42},{12,44},{14,46},{16,48}... | collective-permute-start | bytes 1179656 | tf_op jit(solution)/shard_map/ppermute | solution.py:474
  45.4 2.2 %collective-permute-start.1 = (bf16[16,32,128]{2,1,0:T(8,128)(2,1)S(1)}, bf16[16,32,128]{2,1,0:T(8,128)(2,1)S(1)}, u32[]{:S(2)}, u32[]{:S(2)}) collective-permute-start(bf16[16,32,128]{2,1,0:T(8,128)(2,1)S(1)} %slice.4.rest_0_), channel_id=1, source_target_pairs={{0,96},{2,98},{4,100},{6,102},{8,104},{10,106},{12,108},{14,110},{... | collective-permute-start | bytes 393224 | tf_op jit(solution)/shard_map/ppermute | solution.py:450
  47.5 0.1 collective-permute-start.5
  47.6 0.9 collective-permute-start.6
  48.5 0.5 collective-permute-start.7
  49.1 5.4 %all-to-all-done.query_ref = bf16[16,96,128]{2,1,0:T(8,128)(2,1)S(1)} async-done(((bf16[16,96,128]{2,1,0:T(8,128)(2,1)}), bf16[16,96,128]{2,1,0:T(8,128)(2,1)S(1)}, u32[]{:S(2)}, u32[]{:S(2)}) %all-to-all-start) | async-done | bytes 393248 | tf_op jit(solution)/shard_map/all_to_all | solution.py:439
  54.5 4.4 %collective-permute-done.6.rest_6_ = bf16[16,32,128]{2,1,0:T(8,128)(2,1)} collective-permute-done((bf16[16,32,128]{2,1,0:T(8,128)(2,1)S(1)}, bf16[16,32,128]{2,1,0:T(8,128)(2,1)}, u32[]{:S(2)}, u32[]{:S(2)}) %collective-permute-start.6) | collective-permute-done | bytes 131104 | tf_op jit(solution)/shard_map/ppermute | solution.py:450
  58.9 2.8 %collective-permute-done.7.rest_7_ = bf16[16,32,128]{2,1,0:T(8,128)(2,1)} collective-permute-done((bf16[16,32,128]{2,1,0:T(8,128)(2,1)S(1)}, bf16[16,32,128]{2,1,0:T(8,128)(2,1)}, u32[]{:S(2)}, u32[]{:S(2)}) %collective-permute-start.7) | collective-permute-done | bytes 131104 | tf_op jit(solution)/shard_map/ppermute | solution.py:450
  61.7 12.0 %attend.1 = (bf16[8,96,128]{2,1,0:T(8,128)(2,1)S(1)}, f32[4,16,256]{2,1,0:T(8,128)S(1)}, f32[4,96,256]{2,1,0:T(8,128)S(1)}) custom-call(s32[25]{0:T(128)S(1)} %get-tuple-element.14.need, s32[8,8,256]{2,1,0:T(8,128)S(1)} %get-tuple-element.15.low_ref, bf16[32,128]{1,0:T(8,128)(2,1)S(1)} %get-tuple-element.18.sink_ref, ...), custom_call_target="tpu_custom_call" | custom-call | flops 1610612736 | bytes 4194304 | tf_op jit(solution)/shard_map/attend/pallas_call | solution.py:476
  73.8 2.4 %window.1 = bf16[16,96,128]{2,1,0:T(8,128)(2,1)} custom-call(s32[25]{0:T(128)S(1)} %get-tuple-element.14.need, s32[8,8,256]{2,1,0:T(8,128)S(1)} %get-tuple-element.15.low_ref, bf16[16,96,128]{2,1,0:T(8,128)(2,1)S(1)} %all-to-all-done.query_ref, bf16[8,192,128]{2,1,0:T(8,128)(2,1)S(1)} %collective-permute-done.win_ref, ...), custom_call_target="tpu_custom_call" | custom-call | tf_op jit(solution)/shard_map/window/pallas_call | solution.py:496
  76.2 8.2 %all-to-all-start.2 = ((bf16[16,96,128]{2,1,0:T(8,128)(2,1)}), bf16[16,96,128]{2,1,0:T(8,128)(2,1)S(1)}, u32[]{:S(2)}, u32[]{:S(2)}) async-start(bf16[16,96,128]{2,1,0:T(8,128)(2,1)} %window.1), calls=%async_computation.2 | async-start | bytes 786432 | tf_op jit(solution)/shard_map/all_to_all | solution.py:439
  84.4 14.5 %all-to-all-done.2 = bf16[16,96,128]{2,1,0:T(8,128)(2,1)S(1)} async-done(((bf16[16,96,128]{2,1,0:T(8,128)(2,1)}), bf16[16,96,128]{2,1,0:T(8,128)(2,1)S(1)}, u32[]{:S(2)}, u32[]{:S(2)}) %all-to-all-start.2) | async-done | bytes 393248 | tf_op jit(solution)/shard_map/all_to_all | solution.py:439
  98.9 2.7 %project.3 = bf16[1536,128]{1,0:T(8,128)(2,1)S(1)} custom-call(s32[1]{0:T(128)} %bitcast.4.side, bf16[1536,128]{1,0:T(8,128)(2,1)S(1)} %bitcast.5, bf16[1536,3072]{1,0:T(8,128)(2,1)} %w_ref.3), custom_call_target="tpu_custom_call" | custom-call | flops 603979776 | bytes 4718592 | tf_op jit(solution)/shard_map/project/pallas_call | solution.py:375
  101.7 0.9 collective-permute-start.8
  102.6 2.8 %project.2 = f32[1536,128]{1,0:T(8,128)S(1)} custom-call(s32[1]{0:T(128)} %bitcast.side, bf16[1536,128]{1,0:T(8,128)(2,1)S(1)} %bitcast.6, bf16[1536,3072]{1,0:T(8,128)(2,1)} %w_ref.3), custom_call_target="tpu_custom_call" | custom-call | flops 603979776 | bytes 4718592 | tf_op jit(solution)/shard_map/project/pallas_call | solution.py:375
  105.4 8.4 %collective-permute-done.8 = bf16[1536,128]{1,0:T(8,128)(2,1)S(1)} collective-permute-done((bf16[1536,128]{1,0:T(8,128)(2,1)S(1)}, bf16[1536,128]{1,0:T(8,128)(2,1)S(1)}, u32[]{:S(2)}, u32[]{:S(2)}) %collective-permute-start.8) | collective-permute-done | bytes 393248 | tf_op jit(solution)/shard_map/ppermute | solution.py:510
  113.8 0.8 add_convert_fusion
  (12 shorter events, 0.0 us)
Async XLA Ops:
  2.4 34.5 %all-to-all-start.1 = ((bf16[16,224,128]{2,1,0:T(8,128)(2,1)}), bf16[16,224,128]{2,1,0:T(8,128)(2,1)S(1)}, u32[]{:S(2)}, u32[]{:S(2)}) async-start(bf16[16,224,128]{2,1,0:T(8,128)(2,1)} %pack.1), calls=%async_computation.1 | async-start | bytes 1835008 | tf_op jit(solution)/shard_map/all_to_all | solution.py:439
  11.6 1.0 copy-start
  12.6 0.7 copy-start.1
  13.3 0.7 copy-start.2
  14.1 0.7 copy-start.3
  14.7 0.7 copy-start.4
  36.9 17.6 %all-to-all-start = ((bf16[16,96,128]{2,1,0:T(8,128)(2,1)}), bf16[16,96,128]{2,1,0:T(8,128)(2,1)S(1)}, u32[]{:S(2)}, u32[]{:S(2)}) async-start(bf16[16,96,128]{2,1,0:T(8,128)(2,1)} %get-tuple-element.16), calls=%async_computation | async-start | bytes 786432 | tf_op jit(solution)/shard_map/all_to_all | solution.py:439
  40.4 7.2 %collective-permute-start.4 = (bf16[16,32,128]{2,1,0:T(8,128)(2,1)S(1)}, bf16[16,32,128]{2,1,0:T(8,128)(2,1)S(1)}, u32[]{:S(2)}, u32[]{:S(2)}) collective-permute-start(bf16[16,32,128]{2,1,0:T(8,128)(2,1)S(1)} %slice.4.rest_0_), channel_id=1, source_target_pairs={{0,128},{2,130},{4,132},{6,134},{8,136},{10,138},{12,140},{14,142}... | collective-permute-start | bytes 393224 | tf_op jit(solution)/shard_map/ppermute | solution.py:450
  41.0 6.6 %collective-permute-start.2 = (bf16[16,32,128]{2,1,0:T(8,128)(2,1)S(1)}, bf16[16,32,128]{2,1,0:T(8,128)(2,1)S(1)}, u32[]{:S(2)}, u32[]{:S(2)}) collective-permute-start(bf16[16,32,128]{2,1,0:T(8,128)(2,1)S(1)} %slice.4.rest_0_), channel_id=1, source_target_pairs={{0,64},{2,66},{4,68},{6,70},{8,72},{10,74},{12,76},{14,78},{16,80}... | collective-permute-start | bytes 393224 | tf_op jit(solution)/shard_map/ppermute | solution.py:450
  42.0 6.6 %collective-permute-start.3 = (bf16[16,32,128]{2,1,0:T(8,128)(2,1)S(1)}, bf16[16,32,128]{2,1,0:T(8,128)(2,1)S(1)}, u32[]{:S(2)}, u32[]{:S(2)}) collective-permute-start(bf16[16,32,128]{2,1,0:T(8,128)(2,1)S(1)} %slice.4.rest_0_), channel_id=1, source_target_pairs={{0,32},{2,34},{4,36},{6,38},{8,40},{10,42},{12,44},{14,46},{16,48}... | collective-permute-start | bytes 393224 | tf_op jit(solution)/shard_map/ppermute | solution.py:450
  44.1 29.7 %collective-permute-start = (bf16[8,192,128]{2,1,0:T(8,128)(2,1)S(1)}, bf16[8,192,128]{2,1,0:T(8,128)(2,1)S(1)}, u32[]{:S(2)}, u32[]{:S(2)}) collective-permute-start(bf16[8,192,128]{2,1,0:T(8,128)(2,1)S(1)} %get-tuple-element.17), channel_id=1, source_target_pairs={{0,32},{2,34},{4,36},{6,38},{8,40},{10,42},{12,44},{14,46},{16,48}... | collective-permute-start | bytes 1179656 | tf_op jit(solution)/shard_map/ppermute | solution.py:474
  45.4 9.2 %collective-permute-start.1 = (bf16[16,32,128]{2,1,0:T(8,128)(2,1)S(1)}, bf16[16,32,128]{2,1,0:T(8,128)(2,1)S(1)}, u32[]{:S(2)}, u32[]{:S(2)}) collective-permute-start(bf16[16,32,128]{2,1,0:T(8,128)(2,1)S(1)} %slice.4.rest_0_), channel_id=1, source_target_pairs={{0,96},{2,98},{4,100},{6,102},{8,104},{10,106},{12,108},{14,110},{... | collective-permute-start | bytes 393224 | tf_op jit(solution)/shard_map/ppermute | solution.py:450
  47.5 7.0 %collective-permute-start.5 = (bf16[16,32,128]{2,1,0:T(8,128)(2,1)S(1)}, bf16[16,32,128]{2,1,0:T(8,128)(2,1)S(1)}, u32[]{:S(2)}, u32[]{:S(2)}) collective-permute-start(bf16[16,32,128]{2,1,0:T(8,128)(2,1)S(1)} %collective-permute-done.4.rest_4_), channel_id=1, source_target_pairs={{0,96},{2,98},{4,100},{6,102},{8,104},{10,106},{12,108},{14,110},{... | collective-permute-start | bytes 393224 | tf_op jit(solution)/shard_map/ppermute | solution.py:450
  47.6 11.3 %collective-permute-start.6 = (bf16[16,32,128]{2,1,0:T(8,128)(2,1)S(1)}, bf16[16,32,128]{2,1,0:T(8,128)(2,1)}, u32[]{:S(2)}, u32[]{:S(2)}) collective-permute-start(bf16[16,32,128]{2,1,0:T(8,128)(2,1)S(1)} %collective-permute-done.2.rest_2_), channel_id=1, source_target_pairs={{0,128},{2,130},{4,132},{6,134},{8,136},{10,138},{12,140},{14,142}... | collective-permute-start | bytes 393224 | tf_op jit(solution)/shard_map/ppermute | solution.py:450
  48.5 13.2 %collective-permute-start.7 = (bf16[16,32,128]{2,1,0:T(8,128)(2,1)S(1)}, bf16[16,32,128]{2,1,0:T(8,128)(2,1)}, u32[]{:S(2)}, u32[]{:S(2)}) collective-permute-start(bf16[16,32,128]{2,1,0:T(8,128)(2,1)S(1)} %collective-permute-done.3.rest_3_), channel_id=1, source_target_pairs={{0,128},{2,130},{4,132},{6,134},{8,136},{10,138},{12,140},{14,142}... | collective-permute-start | bytes 393224 | tf_op jit(solution)/shard_map/ppermute | solution.py:450
  76.2 22.7 %all-to-all-start.2 = ((bf16[16,96,128]{2,1,0:T(8,128)(2,1)}), bf16[16,96,128]{2,1,0:T(8,128)(2,1)S(1)}, u32[]{:S(2)}, u32[]{:S(2)}) async-start(bf16[16,96,128]{2,1,0:T(8,128)(2,1)} %window.1), calls=%async_computation.2 | async-start | bytes 786432 | tf_op jit(solution)/shard_map/all_to_all | solution.py:439
  101.7 12.1 %collective-permute-start.8 = (bf16[1536,128]{1,0:T(8,128)(2,1)S(1)}, bf16[1536,128]{1,0:T(8,128)(2,1)S(1)}, u32[]{:S(2)}, u32[]{:S(2)}) collective-permute-start(bf16[1536,128]{1,0:T(8,128)(2,1)S(1)} %project.3), channel_id=1, source_target_pairs={{0,1},{1,0},{2,3},{3,2},{4,5},{5,4},{6,7},{7,6},{8,9},{9,8},{10,11... | collective-permute-start | bytes 1179656 | tf_op jit(solution)/shard_map/ppermute | solution.py:510

commit v3 on v2

--- a/solution.py
+++ b/solution.py
@@ -369,9 +369,8 @@
             out_ref[...] = (sum_ref[...] + part).T.astype(out_ref.dtype)
 
 
-def project(side, attn_t, w_out, dtype):
+def project(side, attn_t, w_out, dtype, features):
     width, rows = attn_t.shape
-    features = w_out.shape[1] // 2
     return pl.pallas_call(
         project_kernel,
         out_shape=jax.ShapeDtypeStruct((features, rows), dtype),
@@ -506,9 +505,13 @@
         name="window",
     )(need, lows, mine_q, window, upper, stats, sums)
     attn_t = trade(attn, members).reshape(width, rows)
-    give = project(1 - half, attn_t, w_out, jnp.bfloat16)
-    got = lax.ppermute(give, "head", [(0, 1), (1, 0)])
-    keep = project(half, attn_t, w_out, jnp.float32)
+    features = w_out.shape[1] // 2
+    got = []
+    for n in range(2):
+        give = project(2 * (1 - half) + n, attn_t, w_out, jnp.bfloat16, features // 2)
+        got.append(lax.ppermute(give, "head", [(0, 1), (1, 0)]))
+    got = jnp.concatenate(got, axis=0)
+    keep = project(half, attn_t, w_out, jnp.float32, features)
     return (keep + got.astype(jnp.float32)).astype(jnp.bfloat16)
 
 

time: 115 us -> 115 us (level)
  the two profiles are of different devices: /device:TPU:31 before, /device:TPU:27 now
where the time goes in v3:
time: 115 us; the launch traced here: 114 us
  waiting for transfers between devices  51 us (44%)
  starting transfers between devices  32.2 us (28%)
  Pallas kernels  26.5 us (23%)
  local copies, waits for them, and re-layouts  3.79 us (3%)
    all_to_all x3, waiting for transfers between devices, trade(): lax.all_to_all(array, 'seq', 0, 0, axis_index_groups=groups, tiled=True)  39.4 us
    all_to_all x3, starting transfers between devices, trade(): lax.all_to_all(array, 'seq', 0, 0, axis_index_groups=groups, tiled=True)  20.8 us
    pallas_call x1, Pallas kernels, shards(): pl.pallas_call(functools.partial(attend_kernel, rings=rings), out_shape=(...  12 us
    pallas_call x3, Pallas kernels, project(): pl.pallas_call(project_kernel, out_shape=jax.ShapeDtypeStruct((features,...  7.08 us
    ppermute x7, starting transfers between devices, send(): return lax.ppermute(array, 'seq', pairs)  6.92 us
    ppermute x7, waiting for transfers between devices, send(): return lax.ppermute(array, 'seq', pairs)  6.9 us
    ppermute x2, waiting for transfers between devices, shards(): got.append(lax.ppermute(give, 'head', [(0, 1), (1, 0)]))  4.72 us
    unnamed x10, local copies, waits for them, and re-layouts  3.78 us
  transfers between devices with their start and end apart: 13, of which 6 were waited for; matrix products, arithmetic and copies ran while one was open for 0% of the time, Pallas kernels for 17%

profile of v3, /device:TPU:27, one launch (start us, length us, event | category | flops | bytes accessed | tf_op | source)
XLA Modules:
  0.0 114.4 jit_solution(8302636731790476902)
XLA Ops:
  0.0 2.4 %pack.1 = bf16[16,224,128]{2,1,0:T(8,128)(2,1)} custom-call(bf16[128,1536]{1,0:T(8,128)(2,1)} %k_ref.1, bf16[128,1536]{1,0:T(8,128)(2,1)} %v_ref.1, bf16[16,1536]{1,0:T(8,128)(2,1)} %ck_ref.1, bf16[16,1536]{1,0:T(8,128)(2,1)} %cv_ref.1), custom_call_target="tpu_custom_call" | custom-call | tf_op jit(solution)/shard_map/pack/pallas_call | solution.py:411
  2.4 9.2 %all-to-all-start.1 = ((bf16[16,224,128]{2,1,0:T(8,128)(2,1)}), bf16[16,224,128]{2,1,0:T(8,128)(2,1)S(1)}, u32[]{:S(2)}, u32[]{:S(2)}) async-start(bf16[16,224,128]{2,1,0:T(8,128)(2,1)} %pack.1), calls=%async_computation.1 | async-start | bytes 1835008 | tf_op jit(solution)/shard_map/all_to_all | solution.py:438
  11.6 1.0 copy-done
  12.6 0.7 copy-done.1
  13.3 0.7 copy-done.2
  14.1 0.7 copy-done.3
  14.7 0.7 copy-done.4
  15.4 2.4 %pack_query.1 = (bf16[16,96,128]{2,1,0:T(8,128)(2,1)}, bf16[32,128]{1,0:T(8,128)(2,1)S(1)}, s32[8,8,256]{2,1,0:T(8,128)S(1)}, s32[25]{0:T(128)S(1)}) custom-call(s32[2]{0:T(128)S(1)} %pad_add_fusion.place, s32[32]{0:T(128)S(1)} %copy-done.3, s32[32]{0:T(128)S(1)} %copy-done.4, bf16[128,1536]{1,0:T(8,128)(2,1)S(1)} %copy-done, bf16[8,1536]{1,0:T(8,128)(2,1)S(1)} %copy-done.1, ...), custom_call_target="tpu_custom_call" | custom-call | flops 1048576 | bytes 2097152 | tf_op jit(solution)/shard_map/pack_query/pallas_call | solution.py:421
  17.8 19.1 %all-to-all-done.1.own_ref = bf16[16,224,128]{2,1,0:T(8,128)(2,1)S(1)} async-done(((bf16[16,224,128]{2,1,0:T(8,128)(2,1)}), bf16[16,224,128]{2,1,0:T(8,128)(2,1)S(1)}, u32[]{:S(2)}, u32[]{:S(2)}) %all-to-all-start.1) | async-done | bytes 917536 | tf_op jit(solution)/shard_map/all_to_all | solution.py:438
  36.9 3.5 %all-to-all-start = ((bf16[16,96,128]{2,1,0:T(8,128)(2,1)}), bf16[16,96,128]{2,1,0:T(8,128)(2,1)S(1)}, u32[]{:S(2)}, u32[]{:S(2)}) async-start(bf16[16,96,128]{2,1,0:T(8,128)(2,1)} %get-tuple-element.16), calls=%async_computation | async-start | bytes 786432 | tf_op jit(solution)/shard_map/all_to_all | solution.py:438
  40.4 0.3 collective-permute-start.4
  40.7 1.0 collective-permute-start.2
  41.7 1.9 %collective-permute-start.3 = (bf16[16,32,128]{2,1,0:T(8,128)(2,1)S(1)}, bf16[16,32,128]{2,1,0:T(8,128)(2,1)S(1)}, u32[]{:S(2)}, u32[]{:S(2)}) collective-permute-start(bf16[16,32,128]{2,1,0:T(8,128)(2,1)S(1)} %slice.4.rest_0_), channel_id=1, source_target_pairs={{0,32},{2,34},{4,36},{6,38},{8,40},{10,42},{12,44},{14,46},{16,48}... | collective-permute-start | bytes 393224 | tf_op jit(solution)/shard_map/ppermute | solution.py:449
  43.6 0.2 prep.1
  43.8 1.3 %collective-permute-start = (bf16[8,192,128]{2,1,0:T(8,128)(2,1)S(1)}, bf16[8,192,128]{2,1,0:T(8,128)(2,1)S(1)}, u32[]{:S(2)}, u32[]{:S(2)}) collective-permute-start(bf16[8,192,128]{2,1,0:T(8,128)(2,1)S(1)} %get-tuple-element.17), channel_id=1, source_target_pairs={{0,32},{2,34},{4,36},{6,38},{8,40},{10,42},{12,44},{14,46},{16,48}... | collective-permute-start | bytes 1179656 | tf_op jit(solution)/shard_map/ppermute | solution.py:473
  45.1 2.2 %collective-permute-start.1 = (bf16[16,32,128]{2,1,0:T(8,128)(2,1)S(1)}, bf16[16,32,128]{2,1,0:T(8,128)(2,1)S(1)}, u32[]{:S(2)}, u32[]{:S(2)}) collective-permute-start(bf16[16,32,128]{2,1,0:T(8,128)(2,1)S(1)} %slice.4.rest_0_), channel_id=1, source_target_pairs={{0,96},{2,98},{4,100},{6,102},{8,104},{10,106},{12,108},{14,110},{... | collective-permute-start | bytes 393224 | tf_op jit(solution)/shard_map/ppermute | solution.py:449
  47.3 1.2 %collective-permute-start.6 = (bf16[16,32,128]{2,1,0:T(8,128)(2,1)S(1)}, bf16[16,32,128]{2,1,0:T(8,128)(2,1)}, u32[]{:S(2)}, u32[]{:S(2)}) collective-permute-start(bf16[16,32,128]{2,1,0:T(8,128)(2,1)S(1)} %collective-permute-done.2.rest_2_), channel_id=1, source_target_pairs={{0,128},{2,130},{4,132},{6,134},{8,136},{10,138},{12,140},{14,142}... | collective-permute-start | bytes 393224 | tf_op jit(solution)/shard_map/ppermute | solution.py:449
  48.5 0.3 collective-permute-start.7
  48.8 5.7 %all-to-all-done.query_ref = bf16[16,96,128]{2,1,0:T(8,128)(2,1)S(1)} async-done(((bf16[16,96,128]{2,1,0:T(8,128)(2,1)}), bf16[16,96,128]{2,1,0:T(8,128)(2,1)S(1)}, u32[]{:S(2)}, u32[]{:S(2)}) %all-to-all-start) | async-done | bytes 393248 | tf_op jit(solution)/shard_map/all_to_all | solution.py:438
  54.5 4.1 %collective-permute-done.6.rest_6_ = bf16[16,32,128]{2,1,0:T(8,128)(2,1)} collective-permute-done((bf16[16,32,128]{2,1,0:T(8,128)(2,1)S(1)}, bf16[16,32,128]{2,1,0:T(8,128)(2,1)}, u32[]{:S(2)}, u32[]{:S(2)}) %collective-permute-start.6) | collective-permute-done | bytes 131104 | tf_op jit(solution)/shard_map/ppermute | solution.py:449
  58.6 2.8 %collective-permute-done.7.rest_7_ = bf16[16,32,128]{2,1,0:T(8,128)(2,1)} collective-permute-done((bf16[16,32,128]{2,1,0:T(8,128)(2,1)S(1)}, bf16[16,32,128]{2,1,0:T(8,128)(2,1)}, u32[]{:S(2)}, u32[]{:S(2)}) %collective-permute-start.7) | collective-permute-done | bytes 131104 | tf_op jit(solution)/shard_map/ppermute | solution.py:449
  61.4 12.0 %attend.1 = (bf16[8,96,128]{2,1,0:T(8,128)(2,1)S(1)}, f32[4,16,256]{2,1,0:T(8,128)S(1)}, f32[4,96,256]{2,1,0:T(8,128)S(1)}) custom-call(s32[25]{0:T(128)S(1)} %get-tuple-element.14.need, s32[8,8,256]{2,1,0:T(8,128)S(1)} %get-tuple-element.15.low_ref, bf16[32,128]{1,0:T(8,128)(2,1)S(1)} %get-tuple-element.18.sink_ref, ...), custom_call_target="tpu_custom_call" | custom-call | flops 1610612736 | bytes 4194304 | tf_op jit(solution)/shard_map/attend/pallas_call | solution.py:475
  73.5 2.4 %window.1 = bf16[16,96,128]{2,1,0:T(8,128)(2,1)} custom-call(s32[25]{0:T(128)S(1)} %get-tuple-element.14.need, s32[8,8,256]{2,1,0:T(8,128)S(1)} %get-tuple-element.15.low_ref, bf16[16,96,128]{2,1,0:T(8,128)(2,1)S(1)} %all-to-all-done.query_ref, bf16[8,192,128]{2,1,0:T(8,128)(2,1)S(1)} %collective-permute-done.win_ref, ...), custom_call_target="tpu_custom_call" | custom-call | tf_op jit(solution)/shard_map/window/pallas_call | solution.py:495
  75.9 8.2 %all-to-all-start.2 = ((bf16[16,96,128]{2,1,0:T(8,128)(2,1)}), bf16[16,96,128]{2,1,0:T(8,128)(2,1)S(1)}, u32[]{:S(2)}, u32[]{:S(2)}) async-start(bf16[16,96,128]{2,1,0:T(8,128)(2,1)} %window.1), calls=%async_computation.2 | async-start | bytes 786432 | tf_op jit(solution)/shard_map/all_to_all | solution.py:438
  84.1 14.5 %all-to-all-done.2 = bf16[16,96,128]{2,1,0:T(8,128)(2,1)S(1)} async-done(((bf16[16,96,128]{2,1,0:T(8,128)(2,1)}), bf16[16,96,128]{2,1,0:T(8,128)(2,1)S(1)}, u32[]{:S(2)}, u32[]{:S(2)}) %all-to-all-start.2) | async-done | bytes 393248 | tf_op jit(solution)/shard_map/all_to_all | solution.py:438
  98.6 2.1 %project.5 = bf16[768,128]{1,0:T(8,128)(2,1)S(1)} custom-call(s32[1]{0:T(128)} %bitcast.5.side, bf16[1536,128]{1,0:T(8,128)(2,1)S(1)} %bitcast.6, bf16[1536,3072]{1,0:T(8,128)(2,1)} %w_ref.5), custom_call_target="tpu_custom_call" | custom-call | flops 301989888 | bytes 2359296 | tf_op jit(solution)/shard_map/project/pallas_call | solution.py:374
  100.8 2.2 %collective-permute-start.9 = (bf16[768,128]{1,0:T(8,128)(2,1)S(1)}, bf16[768,128]{1,0:T(8,128)(2,1)S(1)}, u32[]{:S(2)}, u32[]{:S(2)}) collective-permute-start(bf16[768,128]{1,0:T(8,128)(2,1)S(1)} %project.5), channel_id=1, source_target_pairs={{0,1},{1,0},{2,3},{3,2},{4,5},{5,4},{6,7},{7,6},{8,9},{9,8},{10,11... | collective-permute-start | bytes 589832 | tf_op jit(solution)/shard_map/ppermute | solution.py:512
  103.0 2.1 %project.4 = bf16[768,128]{1,0:T(8,128)(2,1)S(1)} custom-call(s32[1]{0:T(128)} %bitcast.4.side, bf16[1536,128]{1,0:T(8,128)(2,1)S(1)} %bitcast.7, bf16[1536,3072]{1,0:T(8,128)(2,1)} %w_ref.5), custom_call_target="tpu_custom_call" | custom-call | flops 301989888 | bytes 2359296 | tf_op jit(solution)/shard_map/project/pallas_call | solution.py:374
  105.1 0.9 collective-permute-start.8
  106.1 2.8 %project.3 = f32[1536,128]{1,0:T(8,128)S(1)} custom-call(s32[1]{0:T(128)} %bitcast.side, bf16[1536,128]{1,0:T(8,128)(2,1)S(1)} %bitcast.8, bf16[1536,3072]{1,0:T(8,128)(2,1)} %w_ref.5), custom_call_target="tpu_custom_call" | custom-call | flops 603979776 | bytes 4718592 | tf_op jit(solution)/shard_map/project/pallas_call | solution.py:374
  108.9 4.7 %collective-permute-done.8 = bf16[768,128]{1,0:T(8,128)(2,1)S(1)} collective-permute-done((bf16[768,128]{1,0:T(8,128)(2,1)S(1)}, bf16[768,128]{1,0:T(8,128)(2,1)S(1)}, u32[]{:S(2)}, u32[]{:S(2)}) %collective-permute-start.8) | collective-permute-done | bytes 196640 | tf_op jit(solution)/shard_map/ppermute | solution.py:512
  113.6 0.8 add_convert_fusion
  (15 shorter events, 0.2 us)
Async XLA Ops:
  2.4 34.5 %all-to-all-start.1 = ((bf16[16,224,128]{2,1,0:T(8,128)(2,1)}), bf16[16,224,128]{2,1,0:T(8,128)(2,1)S(1)}, u32[]{:S(2)}, u32[]{:S(2)}) async-start(bf16[16,224,128]{2,1,0:T(8,128)(2,1)} %pack.1), calls=%async_computation.1 | async-start | bytes 1835008 | tf_op jit(solution)/shard_map/all_to_all | solution.py:438
  11.6 1.0 copy-start
  12.6 0.7 copy-start.1
  13.3 0.7 copy-start.2
  14.1 0.7 copy-start.3
  14.7 0.7 copy-start.4
  36.9 17.6 %all-to-all-start = ((bf16[16,96,128]{2,1,0:T(8,128)(2,1)}), bf16[16,96,128]{2,1,0:T(8,128)(2,1)S(1)}, u32[]{:S(2)}, u32[]{:S(2)}) async-start(bf16[16,96,128]{2,1,0:T(8,128)(2,1)} %get-tuple-element.16), calls=%async_computation | async-start | bytes 786432 | tf_op jit(solution)/shard_map/all_to_all | solution.py:438
  40.4 6.9 %collective-permute-start.4 = (bf16[16,32,128]{2,1,0:T(8,128)(2,1)S(1)}, bf16[16,32,128]{2,1,0:T(8,128)(2,1)S(1)}, u32[]{:S(2)}, u32[]{:S(2)}) collective-permute-start(bf16[16,32,128]{2,1,0:T(8,128)(2,1)S(1)} %slice.4.rest_0_), channel_id=1, source_target_pairs={{0,128},{2,130},{4,132},{6,134},{8,136},{10,138},{12,140},{14,142}... | collective-permute-start | bytes 393224 | tf_op jit(solution)/shard_map/ppermute | solution.py:449
  40.7 6.6 %collective-permute-start.2 = (bf16[16,32,128]{2,1,0:T(8,128)(2,1)S(1)}, bf16[16,32,128]{2,1,0:T(8,128)(2,1)S(1)}, u32[]{:S(2)}, u32[]{:S(2)}) collective-permute-start(bf16[16,32,128]{2,1,0:T(8,128)(2,1)S(1)} %slice.4.rest_0_), channel_id=1, source_target_pairs={{0,64},{2,66},{4,68},{6,70},{8,72},{10,74},{12,76},{14,78},{16,80}... | collective-permute-start | bytes 393224 | tf_op jit(solution)/shard_map/ppermute | solution.py:449
  41.7 6.9 %collective-permute-start.3 = (bf16[16,32,128]{2,1,0:T(8,128)(2,1)S(1)}, bf16[16,32,128]{2,1,0:T(8,128)(2,1)S(1)}, u32[]{:S(2)}, u32[]{:S(2)}) collective-permute-start(bf16[16,32,128]{2,1,0:T(8,128)(2,1)S(1)} %slice.4.rest_0_), channel_id=1, source_target_pairs={{0,32},{2,34},{4,36},{6,38},{8,40},{10,42},{12,44},{14,46},{16,48}... | collective-permute-start | bytes 393224 | tf_op jit(solution)/shard_map/ppermute | solution.py:449
  43.8 29.7 %collective-permute-start = (bf16[8,192,128]{2,1,0:T(8,128)(2,1)S(1)}, bf16[8,192,128]{2,1,0:T(8,128)(2,1)S(1)}, u32[]{:S(2)}, u32[]{:S(2)}) collective-permute-start(bf16[8,192,128]{2,1,0:T(8,128)(2,1)S(1)} %get-tuple-element.17), channel_id=1, source_target_pairs={{0,32},{2,34},{4,36},{6,38},{8,40},{10,42},{12,44},{14,46},{16,48}... | collective-permute-start | bytes 1179656 | tf_op jit(solution)/shard_map/ppermute | solution.py:473
  45.1 9.5 %collective-permute-start.1 = (bf16[16,32,128]{2,1,0:T(8,128)(2,1)S(1)}, bf16[16,32,128]{2,1,0:T(8,128)(2,1)S(1)}, u32[]{:S(2)}, u32[]{:S(2)}) collective-permute-start(bf16[16,32,128]{2,1,0:T(8,128)(2,1)S(1)} %slice.4.rest_0_), channel_id=1, source_target_pairs={{0,96},{2,98},{4,100},{6,102},{8,104},{10,106},{12,108},{14,110},{... | collective-permute-start | bytes 393224 | tf_op jit(solution)/shard_map/ppermute | solution.py:449
  47.2 7.3 %collective-permute-start.5 = (bf16[16,32,128]{2,1,0:T(8,128)(2,1)S(1)}, bf16[16,32,128]{2,1,0:T(8,128)(2,1)S(1)}, u32[]{:S(2)}, u32[]{:S(2)}) collective-permute-start(bf16[16,32,128]{2,1,0:T(8,128)(2,1)S(1)} %collective-permute-done.4.rest_4_), channel_id=1, source_target_pairs={{0,96},{2,98},{4,100},{6,102},{8,104},{10,106},{12,108},{14,110},{... | collective-permute-start | bytes 393224 | tf_op jit(solution)/shard_map/ppermute | solution.py:449
  47.3 11.3 %collective-permute-start.6 = (bf16[16,32,128]{2,1,0:T(8,128)(2,1)S(1)}, bf16[16,32,128]{2,1,0:T(8,128)(2,1)}, u32[]{:S(2)}, u32[]{:S(2)}) collective-permute-start(bf16[16,32,128]{2,1,0:T(8,128)(2,1)S(1)} %collective-permute-done.2.rest_2_), channel_id=1, source_target_pairs={{0,128},{2,130},{4,132},{6,134},{8,136},{10,138},{12,140},{14,142}... | collective-permute-start | bytes 393224 | tf_op jit(solution)/shard_map/ppermute | solution.py:449
  48.5 12.9 %collective-permute-start.7 = (bf16[16,32,128]{2,1,0:T(8,128)(2,1)S(1)}, bf16[16,32,128]{2,1,0:T(8,128)(2,1)}, u32[]{:S(2)}, u32[]{:S(2)}) collective-permute-start(bf16[16,32,128]{2,1,0:T(8,128)(2,1)S(1)} %collective-permute-done.3.rest_3_), channel_id=1, source_target_pairs={{0,128},{2,130},{4,132},{6,134},{8,136},{10,138},{12,140},{14,142}... | collective-permute-start | bytes 393224 | tf_op jit(solution)/shard_map/ppermute | solution.py:449
  75.9 22.7 %all-to-all-start.2 = ((bf16[16,96,128]{2,1,0:T(8,128)(2,1)}), bf16[16,96,128]{2,1,0:T(8,128)(2,1)S(1)}, u32[]{:S(2)}, u32[]{:S(2)}) async-start(bf16[16,96,128]{2,1,0:T(8,128)(2,1)} %window.1), calls=%async_computation.2 | async-start | bytes 786432 | tf_op jit(solution)/shard_map/all_to_all | solution.py:438
  100.8 8.1 %collective-permute-start.9 = (bf16[768,128]{1,0:T(8,128)(2,1)S(1)}, bf16[768,128]{1,0:T(8,128)(2,1)S(1)}, u32[]{:S(2)}, u32[]{:S(2)}) collective-permute-start(bf16[768,128]{1,0:T(8,128)(2,1)S(1)} %project.5), channel_id=1, source_target_pairs={{0,1},{1,0},{2,3},{3,2},{4,5},{5,4},{6,7},{7,6},{8,9},{9,8},{10,11... | collective-permute-start | bytes 589832 | tf_op jit(solution)/shard_map/ppermute | solution.py:512
  105.1 8.5 %collective-permute-start.8 = (bf16[768,128]{1,0:T(8,128)(2,1)S(1)}, bf16[768,128]{1,0:T(8,128)(2,1)S(1)}, u32[]{:S(2)}, u32[]{:S(2)}) collective-permute-start(bf16[768,128]{1,0:T(8,128)(2,1)S(1)} %project.4), channel_id=1, source_target_pairs={{0,1},{1,0},{2,3},{3,2},{4,5},{5,4},{6,7},{7,6},{8,9},{9,8},{10,11... | collective-permute-start | bytes 589832 | tf_op jit(solution)/shard_map/ppermute | solution.py:512
